TPU v7x, 32 devices: a whole 2x2x4 slice. The times are simulated.
32 devices in a mesh: cube: 2 (over y), row: 4 (over x, core), col: 4 (over z).
Axes of the slice: x: 2, y: 2, z: 4, core: 2. Of those that a mesh axis runs over, the one named last changes fastest.
Arguments:
- child_panel: bfloat16 [2, 6144, 256], P('cube', ('row', 'col')), may hold values from -0.75 to 0.75
- child_inverse: float32 [2, 256, 256], P('cube')
- child_trailing: bfloat16 [2, 6144, 6144], P('cube', ('row', 'col')), may hold values from -6 to 6
- child_pattern: int32 [2, 48], P('cube'), may hold values 0 or 1
- child_map: int32 [2, 48], replicated, may hold values from 0 to 95, as said below
- parent_panel: bfloat16 [2, 6144, 256], P('cube', ('row', 'col')), may hold values from -0.75 to 0.75
- parent_inverse: float32 [1, 256, 256], replicated
- parent_trailing: bfloat16 [2, 6144, 12288], P('cube', ('row', 'col')), may hold values from -6 to 6
- parent_pattern: int32 [1, 96], replicated, may hold values 0 or 1
Outputs:
- parent_update: bfloat16 [2, 6144, 12288], P('cube', ('row', 'col'))
Inputs may be any that keep to these rules, and one draw needn't show every extreme that they name: With p = i // 3, child_map[c, i] is one of the blocks h * 48 + p * 3 + k, h in 0 and 1, k from 0 to 2; a child's blocks land on distinct parent blocks.
All inputs are finite; a program needn't handle non-finite values. No bound on the sum of `child_pattern` on one device may be relied on, other than what follows from the above.
Results may differ from a plain program's by a relative error of at most 0.0042.
Values may be sent and summed in bfloat16 or wider, within the bound.
No kernel may reach another device: no remote copies, remote signals or barrier semaphores. Data moves between devices by JAX's collectives and lax.ppermute only.
A program may use at most 192 MiB of HBM per device.

v0:
```python
import jax
import jax.numpy as jnp
from jax import lax
from jax.sharding import PartitionSpec as P

BLOCK = 128


def from_partner(array, axis, apart):
    return lax.ppermute(array, axis, [(i, i ^ 1 << apart) for i in range(lax.axis_size(axis))])


def row_mask(pattern_row, start, how_many):
    window = lax.dynamic_slice_in_dim(pattern_row, start, how_many)
    return jnp.repeat(window, BLOCK).astype(jnp.bfloat16)[:, None]


def one_hot(mapping, extent):
    return (mapping[:, None] == jnp.arange(extent, dtype=jnp.int32)[None, :]).astype(jnp.bfloat16)


def map_columns(values, table):
    row_count = values.shape[0]
    blocks = values.reshape(row_count, table.shape[0], BLOCK)
    shifted = jnp.einsum("rib,ip->rpb", blocks, table, preferred_element_type=jnp.float32)
    return shifted.reshape(row_count, table.shape[1] * BLOCK)


def map_rows(values, table):
    column_count = values.shape[1]
    blocks = values.reshape(table.shape[0], BLOCK, column_count)
    shifted = jnp.einsum("iaw,ip->paw", blocks, table, preferred_element_type=jnp.float32)
    return shifted.reshape(table.shape[1] * BLOCK, column_count)


def contribution(trailing, own_panel, whole_panel, inverse):
    left_factor = jnp.dot(
        own_panel.astype(jnp.float32), inverse, precision=lax.Precision.HIGHEST
    ).astype(jnp.bfloat16)
    update = lax.dot_general(
        left_factor, whole_panel, (((1,), (1,)), ((), ())), preferred_element_type=jnp.float32
    )
    return trailing.astype(jnp.float32) - update


def local(
    child_panel,
    child_inverse,
    child_trailing,
    child_pattern,
    child_map,
    parent_panel,
    parent_inverse,
    parent_trailing,
    parent_pattern,
):
    position = lax.axis_index(("row", "col"))
    cube_index = lax.axis_index("cube")
    half_bit = cube_index % 2
    parent = cube_index // 2
    parent_blocks = parent_pattern.shape[1]
    half_rows = parent_trailing.shape[1] * lax.axis_size(("row", "col"))
    panel_piece = child_panel[0]
    blocks_here = panel_piece.shape[0] // BLOCK
    own_panel = panel_piece * row_mask(child_pattern[0], position * blocks_here, blocks_here)
    whole_panel = lax.all_gather(own_panel, ("row", "col"), axis=0, tiled=True)
    schur_rows = contribution(child_trailing[0], own_panel, whole_panel, child_inverse[0]).astype(
        jnp.bfloat16
    )
    own_map = lax.dynamic_index_in_dim(child_map, cube_index, 0, keepdims=False)
    own_table = one_hot(own_map, parent_blocks)
    widened = map_columns(schur_rows, own_table).astype(jnp.bfloat16)
    spread = lax.all_to_all(widened, ("row", "col"), split_axis=1, concat_axis=0, tiled=True)
    placed = map_rows(spread, own_table).astype(jnp.bfloat16)
    own_half = lax.dynamic_slice_in_dim(placed, half_bit * half_rows, half_rows, 0)
    theirs = lax.dynamic_slice_in_dim(placed, (1 - half_bit) * half_rows, half_rows, 0)
    arrived = from_partner(theirs, "cube", 0)
    summed = (own_half.astype(jnp.float32) + arrived.astype(jnp.float32)).astype(jnp.bfloat16)
    assembled = lax.all_to_all(summed, ("row", "col"), split_axis=0, concat_axis=1, tiled=True)
    parent_piece = parent_panel[0]
    parent_here = parent_piece.shape[0] // BLOCK
    pattern_row = lax.dynamic_index_in_dim(parent_pattern, parent, 0, keepdims=False)
    own_parent = parent_piece * row_mask(
        pattern_row, half_bit * (half_rows // BLOCK) + position * parent_here, parent_here
    )
    half_panel = lax.all_gather(own_parent, ("row", "col"), axis=0, tiled=True)
    other_panel = from_partner(half_panel, "cube", 0)
    whole_parent = jnp.where(
        half_bit == 0,
        jnp.concatenate([half_panel, other_panel], axis=0),
        jnp.concatenate([other_panel, half_panel], axis=0),
    )
    inverse = lax.dynamic_index_in_dim(parent_inverse, parent, 0, keepdims=False)
    result = contribution(parent_trailing[0], own_parent, whole_parent, inverse) + assembled.astype(
        jnp.float32
    )
    return result.astype(jnp.bfloat16)[None]


def solution(mesh):
    in_specs = (
        P("cube", ("row", "col"), None),
        P("cube", None, None),
        P("cube", ("row", "col"), None),
        P("cube", None),
        P(),
        P("cube", ("row", "col"), None),
        P(),
        P("cube", ("row", "col"), None),
        P(),
    )
    out_specs = P("cube", ("row", "col"), None)
    return jax.shard_map(local, mesh=mesh, in_specs=in_specs, out_specs=out_specs, check_vma=False)
```

profile of v0, /device:TPU:0, one launch (start us, length us, event | category | flops | bytes accessed | tf_op | source)
XLA Modules:
  0.0 852.1 jit_solution(2174740888799487291)
XLA Ops:
  6.5 0.8 fusion.29
  7.3 0.1 broadcast_bitcast_fusion
  7.4 1.7 bitcast_multiply_fusion
  9.1 0.0 all-gather.5.cloned.1.call-update
  9.1 0.7 fusion.27
  9.8 1.3 convolution_convert_fusion.1
  11.1 46.5 %all-gather.5.cloned.1.call-done = bf16[6144,256]{1,0:T(8,128)(2,1)} async-done(((bf16[384,256]{1,0:T(8,128)(2,1)}), bf16[6144,256]{1,0:T(8,128)(2,1)}) %all-gather.5.cloned.1.call-update) | async-done | bytes 3145744 | tf_op jit(solution)/shard_map/all_gather | solution.py:66
  57.6 4.7 fusion.11
  62.3 1.3 copy.15
  63.6 5.2 convert_bitcast_fusion.1
  68.8 16.8 %convert_element_type.104 = bf16[384,16,768]{2,1,0:T(8,128)(2,1)} reshape(bf16[384,96,128]{2,1,0:T(8,128)(2,1)} %convert_bitcast_fusion.1) | data formatting | bytes 18874368 | tf_op jit(solution)/shard_map/convert_element_type | solution.py:72
  85.6 10.7 %copy.10 = bf16[384,16,768]{2,0,1:T(8,128)(2,1)} copy(bf16[384,16,768]{2,1,0:T(8,128)(2,1)} %convert_element_type.104) | data formatting | bytes 18874368 | tf_op jit(solution)/shard_map/convert_element_type | solution.py:72
  96.3 5.0 all-to-all-start
  101.3 206.5 %all-to-all-done = bf16[384,16,768]{2,0,1:T(8,128)(2,1)} async-done(((bf16[384,16,768]{2,0,1:T(8,128)(2,1)}), bf16[384,16,768]{2,0,1:T(8,128)(2,1)}, u32[]{:S(2)}, u32[]{:S(2)}) %all-to-all-start) | async-done | bytes 9437216 | tf_op jit(solution)/shard_map/all_to_all | solution.py:73
  307.9 16.0 %convolution_convert_fusion = bf16[96,128,768]{2,0,1:T(8,128)(2,1)} fusion(bf16[48,128,768]{2,1,0:T(8,128)(2,1)} %bitcast.16, s32[48]{0:T(128)S(1)} %fusion.27), kind=kOutput, calls=%fused_computation.6 | convolution fusion | flops 915411456 | bytes 28311744 | tf_op jit(solution)/shard_map/iaw,ip->paw/dot_general | solution.py:32
  323.9 20.2 %copy.12 = bf16[96,128,768]{2,1,0:T(8,128)(2,1)} copy(bf16[96,128,768]{2,0,1:T(8,128)(2,1)} %convolution_convert_fusion) | data formatting | bytes 37748736 | tf_op jit(solution)/shard_map/convert_element_type | solution.py:74
  344.1 8.0 constant_dynamic-slice_fusion
  352.1 1.5 collective-permute-start.1
  353.7 203.2 %collective-permute-done.1 = bf16[6144,768]{1,0:T(8,128)(2,1)} collective-permute-done((bf16[6144,768]{1,0:T(8,128)(2,1)}, bf16[6144,768]{1,0:T(8,128)(2,1)}, u32[]{:S(2)}, u32[]{:S(2)}) %collective-permute-start.1) | collective-permute-done | bytes 9437216 | tf_op jit(solution)/shard_map/ppermute | solution.py:10
  556.9 11.9 %add_convert_fusion = bf16[6144,768]{1,0:T(8,128)(2,1)} fusion(bf16[6144,768]{1,0:T(8,128)(2,1)} %collective-permute-done.1, bf16[12288,768]{1,0:T(8,128)(2,1)} %bitcast.60, s32[]{:T(128)S(6)} %select_n.43), kind=kLoop, calls=%fused_computation.4 | loop fusion | flops 18874368 | bytes 28311556 | tf_op jit(solution)/shard_map/convert_element_type | solution.py:78
  568.8 4.9 all-to-all-start.1
  573.8 0.3 all-gather.3.cloned.1.call-start
  574.1 0.1 fusion.26
  574.1 0.1 broadcast_bitcast_fusion.1
  574.2 0.8 bitcast_multiply_fusion.1
  575.1 157.3 %all-gather.3.cloned.1.call-done = bf16[6144,256]{1,0:T(8,128)(2,1)} async-done(((bf16[384,256]{1,0:T(8,128)(2,1)}), bf16[6144,256]{1,0:T(8,128)(2,1)}) %all-gather.3.cloned.1.call-update) | async-done | bytes 3145744 | tf_op jit(solution)/shard_map/all_gather | solution.py:86
  732.4 1.5 collective-permute-start
  733.9 1.0 convolution_convert_fusion.2
  734.9 64.5 %all-to-all-done.1 = bf16[16,384,768]{2,1,0:T(8,128)(2,1)} async-done(((bf16[16,384,768]{2,1,0:T(8,128)(2,1)}), bf16[16,384,768]{2,1,0:T(8,128)(2,1)}, u32[]{:S(2)}, u32[]{:S(2)}) %all-to-all-start.1) | async-done | bytes 9437216 | tf_op jit(solution)/shard_map/all_to_all | solution.py:79
  799.5 12.2 %convert_bitcast_fusion = f32[16,48,8,768]{3,2,1,0:T(8,128)} fusion(bf16[16,384,768]{2,1,0:T(8,128)(2,1)} %all-to-all-done.1), kind=kLoop, calls=%fused_computation.3 | loop fusion | flops 4718592 | bytes 28311552
  811.7 12.9 %copy.14 = f32[16,48,8,768]{3,2,0,1:T(8,128)} copy(f32[16,48,8,768]{3,2,1,0:T(8,128)} %convert_bitcast_fusion) | data formatting | bytes 37748736 | tf_op jit(solution)/shard_map/convert_element_type | solution.py:94
  824.6 20.6 %fusion.2 = bf16[1,384,12288]{2,1,0:T(8,128)(2,1)} fusion(f32[384,12288]{1,0:T(8,128)} %bitcast.58, bf16[384,256]{1,0:T(8,128)(2,1)} %convolution_convert_fusion.2, bf16[1,384,12288]{2,1,0:T(8,128)(2,1)} %param.16, bf16[6144,256]{1,0:T(8,128)(2,1)} %collective-permute-done, bf16[6144,256]{1,0:T(8,128)(2,1)S(1)} %copy-done.2, pred[]{:T(512)S(6)} %eq.20), kind=kOutput, calls=%fused_computation.5 | convolution fusion | flops 2463105024 | bytes 44236800 | tf_op jit(solution)/shard_map/dot_general | solution.py:40
  (15 shorter events, 0.0 us)
Async XLA Ops:
  6.5 3.3 copy-start
  6.5 51.0 %all-gather.5.cloned.1.call-start = ((), (), s32[]{:S(2)}) async-start(), calls=%async_computation.3 | async-start | bytes 3342336 | tf_op jit(solution)/shard_map/all_gather | solution.py:66
  96.3 211.5 %all-to-all-start = ((bf16[384,16,768]{2,0,1:T(8,128)(2,1)}), bf16[384,16,768]{2,0,1:T(8,128)(2,1)}, u32[]{:S(2)}, u32[]{:S(2)}) async-start(bf16[384,16,768]{2,0,1:T(8,128)(2,1)} %copy.10), calls=%async_computation | async-start | bytes 18874368 | tf_op jit(solution)/shard_map/all_to_all | solution.py:73
  352.1 204.8 %collective-permute-start.1 = (bf16[6144,768]{1,0:T(8,128)(2,1)}, bf16[6144,768]{1,0:T(8,128)(2,1)}, u32[]{:S(2)}, u32[]{:S(2)}) collective-permute-start(bf16[6144,768]{1,0:T(8,128)(2,1)} %constant_dynamic-slice_fusion), channel_id=1, source_target_pairs={{0,16},{16,0},{1,17},{17,1},{2,18},{18,2},{3,19},{19,3},{4,20},{20... | collective-permute-start | bytes 28311560 | tf_op jit(solution)/shard_map/ppermute | solution.py:10
  568.8 5.2 copy-start.5
  568.8 5.4 copy-start.3
  568.8 165.1 %copy-start.4 = (f32[1,256,256]{2,1,0:T(8,128)S(1)}, f32[1,256,256]{2,1,0:T(8,128)}, u32[]{:S(2)}) copy-start(f32[1,256,256]{2,1,0:T(8,128)} %param.15) | copy-start | bytes 786436
  568.8 230.6 %all-to-all-start.1 = ((bf16[16,384,768]{2,1,0:T(8,128)(2,1)}), bf16[16,384,768]{2,1,0:T(8,128)(2,1)}, u32[]{:S(2)}, u32[]{:S(2)}) async-start(bf16[16,384,768]{2,1,0:T(8,128)(2,1)} %bitcast.61), calls=%async_computation.1 | async-start | bytes 18874368 | tf_op jit(solution)/shard_map/all_to_all | solution.py:79
  573.8 158.6 %all-gather.3.cloned.1.call-start = ((), (), s32[]{:S(2)}) async-start(), calls=%async_computation.2 | async-start | bytes 3342336 | tf_op jit(solution)/shard_map/all_gather | solution.py:86
  732.4 92.2 %collective-permute-start = (bf16[6144,256]{1,0:T(8,128)(2,1)}, bf16[6144,256]{1,0:T(8,128)(2,1)}, u32[]{:S(2)}, u32[]{:S(2)}) collective-permute-start(bf16[6144,256]{1,0:T(8,128)(2,1)} %all-gather.3.cloned.1.call-done), channel_id=1, source_target_pairs={{0,16},{16,0},{1,17},{17,1},{2,18},{18,2},{3,19},{19,3},{4,20},{20... | collective-permute-start | bytes 9437192 | tf_op jit(solution)/shard_map/ppermute | solution.py:10
  811.7 12.9 %copy-start.2 = (bf16[6144,256]{1,0:T(8,128)(2,1)S(1)}, bf16[6144,256]{1,0:T(8,128)(2,1)}, u32[]{:S(2)}) copy-start(bf16[6144,256]{1,0:T(8,128)(2,1)} %all-gather.3.cloned.1.call-done) | copy-start | bytes 9437188
  824.6 20.6 %copy-start.1 = (f32[1,256,256]{2,1,0:T(8,128)S(1)}, f32[1,256,256]{2,1,0:T(8,128)}, u32[]{:S(2)}) copy-start(f32[1,256,256]{2,1,0:T(8,128)} %param.10) | copy-start | bytes 786436
Sparse Core Ops, SparseCore 0:
  9.7 47.8 all-gather.4
  576.9 155.3 all-gather.2
where the time goes:
time: 853 us; the launch traced here: 852 us
  waiting for transfers between devices  678 us (79%)
  local copies, waits for them, and re-layouts  70.8 us (8%)
  matrix products  48.9 us (6%)
  other arithmetic  27.5 us (3%)
  between operations  13.5 us (2%)
  starting transfers between devices  13.2 us (2%)
    all_to_all x1, waiting for transfers between devices, local(): lax.all_to_all(widened, ('row', 'col'), split_axis=1, concat_axis=0, tile...  207 us
    ppermute x2, waiting for transfers between devices, from_partner(): lax.ppermute(array, axis, [(i, i ^ 1 << apart) for i in range(lax.axis_si...  203 us
    all_gather x1, waiting for transfers between devices, local(): half_panel = lax.all_gather(own_parent, ('row', 'col'), axis=0, tiled=True)  157 us
    all_to_all x1, waiting for transfers between devices, local(): lax.all_to_all(summed, ('row', 'col'), split_axis=0, concat_axis=1, tiled...  64.5 us
    all_gather x1, waiting for transfers between devices, local(): whole_panel = lax.all_gather(own_panel, ('row', 'col'), axis=0, tiled=True)  46.5 us
    convert_element_type x2, local copies, waits for them, and re-layouts, local(): widened = map_columns(schur_rows, own_table).astype(jnp.bfloat16)  27.5 us
    dot_general x2, matrix products, contribution(): lax.dot_general(left_factor, whole_panel, (((1,), (1,)), ((), ())), prefe...  25.3 us
    convert_element_type x1, local copies, waits for them, and re-layouts, local(): placed = map_rows(spread, own_table).astype(jnp.bfloat16)  20.2 us
  transfers between devices with their start and end apart: 6, of which 5 were waited for; matrix products, arithmetic and copies ran while one was open for 3% of the time, Pallas kernels for 0%

commit v1 on v0

v1 whole, which is shorter than its diff:
```python
import functools
import jax
import jax.numpy as jnp
from jax import lax
from jax.experimental import pallas as pl
from jax.experimental.pallas import tpu as pltpu
from jax.sharding import PartitionSpec as P

BLOCK = 128


def swap_cube(array):
    return lax.ppermute(array, "cube", [(i, i ^ 1) for i in range(lax.axis_size("cube"))])


def masked_rows(panel, pattern_row, start):
    blocks = panel.shape[0] // BLOCK
    window = lax.dynamic_slice_in_dim(pattern_row, start, blocks)
    return panel * jnp.repeat(window, BLOCK).astype(panel.dtype)[:, None]


def left_factor(masked, inverse):
    return jnp.dot(masked.astype(jnp.float32), inverse, precision=lax.Precision.HIGHEST).astype(jnp.bfloat16)


def source_table(mapping, positions, parent_blocks):
    each = mapping.shape[0] // positions
    width = parent_blocks // (2 * positions)
    target = jnp.arange(parent_blocks, dtype=jnp.int32).reshape(2, positions, width)
    hit = mapping.reshape(1, positions, 1, each) == target[..., None]
    return jnp.sum(jnp.where(hit, jnp.arange(1, each + 1, dtype=jnp.int32), 0), axis=-1) - 1


def assemble_chunk(first, windows, per_step, positions, each, width, table, place, lefts, gathered, own, other, trailing, previous):
    rows = own.shape[0]
    span = each * BLOCK
    wide = width * BLOCK
    row_blocks = rows // BLOCK
    zero = row_blocks * each
    steps = windows // per_step

    def kernel(table_ref, place_ref, lefts_ref, gathered_ref, own_ref, other_ref, trailing_ref, *rest):
        out_ref, schur_ref = rest[-2:]
        step = pl.program_id(0)
        half = pl.program_id(1)

        def source(child, which_half, window, k):
            return table_ref[((child * 2 + which_half) * positions + window) * width + k]

        @pl.when(half == 0)
        def _():
            for child, piece in enumerate((own_ref, other_ref)):
                for j in range(per_step):
                    update = lax.dot_general(
                        lefts_ref[child], gathered_ref[j, 2 * child], (((1,), (1,)), ((), ())),
                        preferred_element_type=jnp.float32,
                    )
                    schur = (piece[:, j * span:(j + 1) * span].astype(jnp.float32) - update).astype(jnp.bfloat16)
                    for r in range(row_blocks):
                        for c in range(each):
                            schur_ref[child, j, r * each + c] = schur[r * BLOCK:(r + 1) * BLOCK, c * BLOCK:(c + 1) * BLOCK]
                    schur_ref[child, j, zero] = jnp.zeros((BLOCK, BLOCK), jnp.bfloat16)

        own_half = place_ref[0]
        position = place_ref[1]
        slot = jnp.where(half == own_half, 1, 3)
        for j in range(per_step):
            window = first + step * per_step + j
            update = lax.dot_general(
                lefts_ref[2], gathered_ref[j, slot], (((1,), (1,)), ((), ())), preferred_element_type=jnp.float32
            )
            base = trailing_ref[:, j * wide:(j + 1) * wide].astype(jnp.float32) - update
            for a in range(row_blocks):
                for k in range(width):
                    total = None
                    for child in range(2):
                        r = source(child, own_half, position, a)
                        c = source(child, half, window, k)
                        which = jnp.where((r >= 0) & (c >= 0), r * each + c, zero)
                        block = schur_ref[child, j, which].astype(jnp.float32)
                        total = block if total is None else total + block
                    total = total.astype(jnp.bfloat16).astype(jnp.float32)
                    piece = base[a * BLOCK:(a + 1) * BLOCK, k * BLOCK:(k + 1) * BLOCK] + total
                    at = j * wide + k * BLOCK
                    out_ref[a * BLOCK:(a + 1) * BLOCK, at:at + BLOCK] = piece.astype(jnp.bfloat16)

    start = first // per_step
    halves = positions // per_step
    smem = pl.BlockSpec(memory_space=pltpu.SMEM)
    in_specs = [
        smem,
        smem,
        pl.BlockSpec(lefts.shape, lambda s, h: (0, 0, 0)),
        pl.BlockSpec((per_step,) + gathered.shape[1:], lambda s, h: (start + s, 0, 0, 0)),
        pl.BlockSpec((rows, per_step * span), lambda s, h: (0, start + s)),
        pl.BlockSpec((rows, per_step * span), lambda s, h: (0, s)),
        pl.BlockSpec((rows, per_step * wide), lambda s, h: (0, h * halves + start + s)),
    ]
    operands = [table, place, lefts, gathered, own, other, trailing]
    aliases = {}
    if previous is not None:
        in_specs.append(pl.BlockSpec(memory_space=pl.ANY))
        operands.append(previous)
        aliases = {len(operands) - 1: 0}
    return pl.pallas_call(
        kernel,
        grid=(steps, 2),
        in_specs=in_specs,
        out_specs=pl.BlockSpec((rows, per_step * wide), lambda s, h: (0, h * halves + start + s)),
        out_shape=jax.ShapeDtypeStruct(trailing.shape, jnp.bfloat16),
        scratch_shapes=[pltpu.VMEM((2, per_step, zero + 1, BLOCK, BLOCK), jnp.bfloat16)],
        input_output_aliases=aliases,
        name="assemble",
        compiler_params=pltpu.CompilerParams(vmem_limit_bytes=32 * 1024 * 1024),
    )(*operands)


def local(
    child_panel,
    child_inverse,
    child_trailing,
    child_pattern,
    child_map,
    parent_panel,
    parent_inverse,
    parent_trailing,
    parent_pattern,
):
    positions = lax.axis_size(("row", "col"))
    position = lax.axis_index(("row", "col"))
    cube_index = lax.axis_index("cube")
    half_bit = cube_index % 2
    parent = cube_index // 2
    parent_blocks = parent_pattern.shape[1]
    child_blocks = child_map.shape[1]
    each = child_blocks // positions
    width = parent_blocks // (2 * positions)
    own = child_trailing[0]
    rows = own.shape[0]
    span = each * BLOCK

    own_child = masked_rows(child_panel[0], child_pattern[0], position * each)
    pattern_row = lax.dynamic_index_in_dim(parent_pattern, parent, 0, keepdims=False)
    own_parent = masked_rows(parent_panel[0], pattern_row, half_bit * (parent_blocks // 2) + position * width)
    child_left = left_factor(own_child, child_inverse[0])
    parent_left = left_factor(own_parent, lax.dynamic_index_in_dim(parent_inverse, parent, 0, keepdims=False))

    small = jnp.stack([own_child, own_parent, child_left])
    small_other = swap_cube(small)

    per_step = 2
    sizes = [4, 4, 4, 2, 2] if positions == 16 else [positions]
    others, first = [], 0
    for size in sizes:
        others.append(swap_cube(own[:, first * span:(first + size) * span]))
        first += size

    pieces = jnp.concatenate([small[:2], small_other[:2]])
    gathered = lax.all_gather(pieces, ("row", "col"), axis=0, tiled=False)
    lefts = jnp.stack([child_left, small_other[2], parent_left])

    own_map = lax.dynamic_index_in_dim(child_map, cube_index, 0, keepdims=False)
    other_map = lax.dynamic_index_in_dim(child_map, cube_index ^ 1, 0, keepdims=False)
    table = jnp.stack([source_table(m, positions, parent_blocks) for m in (own_map, other_map)]).reshape(-1)
    place = jnp.stack([half_bit, position]).astype(jnp.int32)

    result, first = None, 0
    for size, other in zip(sizes, others):
        result = assemble_chunk(
            first, size, per_step, positions, each, width, table, place, lefts, gathered, own, other, parent_trailing[0], result
        )
        first += size
    return result[None]


def solution(mesh):
    in_specs = (
        P("cube", ("row", "col"), None),
        P("cube", None, None),
        P("cube", ("row", "col"), None),
        P("cube", None),
        P(),
        P("cube", ("row", "col"), None),
        P(),
        P("cube", ("row", "col"), None),
        P(),
    )
    out_specs = P("cube", ("row", "col"), None)
    return jax.shard_map(local, mesh=mesh, in_specs=in_specs, out_specs=out_specs, check_vma=False)
```

time: 853 us -> 175 us (0.21)
  waiting for transfers between devices: 678 us -> 101 us
  local copies, waits for them, and re-layouts: 70.8 us -> 17.8 us
  matrix products: 48.9 us -> 0.71 us
  Pallas kernels: 0 us -> 28.2 us
  other arithmetic: 27.5 us -> 4.07 us
    all_to_all x2 -> x0, waiting for transfers between devices: 271 us -> none  [the longest x1 207 us: local(): lax.all_to_all(widened, ('row', 'col'), split_axis=1, concat_axis=0, tile...]
    ppermute x2 -> x6, waiting for transfers between devices: 203 us -> 32.1 us  [swap_cube(): lax.ppermute(array, 'cube', [(i, i ^ 1) for i in range(lax.axis_size('cub...]
    all_gather x2 -> x1, waiting for transfers between devices: 204 us -> 69.2 us  [local(): gathered = lax.all_gather(pieces, ('row', 'col'), axis=0, tiled=False)]
    convert_element_type x6 -> x2, local copies, waits for them, and re-layouts: 60.8 us -> 0.15 us  [masked_rows(): return panel * jnp.repeat(window, BLOCK).astype(panel.dtype)[:, None]]
    dot_general x6 -> x2, matrix products: 48.9 us -> 0.71 us  [left_factor(): jnp.dot(masked.astype(jnp.float32), inverse, precision=lax.Precision.HIGH...]
    pallas_call x0 -> x5, Pallas kernels: none -> 28.2 us  [assemble_chunk(): pl.pallas_call(kernel, grid=(steps, 2), in_specs=in_specs, out_specs=pl.B...]
    unnamed x1 -> x0, other arithmetic: 12.2 us -> none
    convert_element_type x3 -> x2, other arithmetic: 12.8 us -> 1.5 us  [masked_rows(): return panel * jnp.repeat(window, BLOCK).astype(panel.dtype)[:, None]]
  transfers between devices with their start and end apart: 6 -> 7, of which waited for: 5 -> 3; matrix products, arithmetic and copies ran while one was open for 3% -> 5% of each run, Pallas kernels for 0% -> 14%
where the time goes in v1:
time: 175 us; the launch traced here: 174 us
  waiting for transfers between devices  101 us (58%)
  Pallas kernels  28.2 us (16%)
  local copies, waits for them, and re-layouts  17.8 us (10%)
  between operations  13.5 us (8%)
  starting transfers between devices  8.83 us (5%)
  other arithmetic  4.07 us (2%)
    all_gather x1, waiting for transfers between devices, local(): gathered = lax.all_gather(pieces, ('row', 'col'), axis=0, tiled=False)  69.2 us
    ppermute x6, waiting for transfers between devices, swap_cube(): lax.ppermute(array, 'cube', [(i, i ^ 1) for i in range(lax.axis_size('cub...  32.1 us
    pallas_call x5, Pallas kernels, assemble_chunk(): pl.pallas_call(kernel, grid=(steps, 2), in_specs=in_specs, out_specs=pl.B...  28.2 us
    unnamed x14, local copies, waits for them, and re-layouts  9.71 us
    ppermute x6, starting transfers between devices, swap_cube(): lax.ppermute(array, 'cube', [(i, i ^ 1) for i in range(lax.axis_size('cub...  8.82 us
    slice x2, local copies, waits for them, and re-layouts, local(): others.append(swap_cube(own[:, first * span:(first + size) * span]))  6.35 us
  transfers between devices with their start and end apart: 7, of which 3 were waited for; matrix products, arithmetic and copies ran while one was open for 5% of the time, Pallas kernels for 14%

profile of v1, /device:TPU:0, one launch (start us, length us, event | category | flops | bytes accessed | tf_op | source)
XLA Modules:
  0.0 174.4 jit_solution(12321519781948313766)
XLA Ops:
  6.5 0.8 fusion.13
  7.4 0.7 fusion.11
  8.2 1.2 broadcast_multiply_fusion
  9.4 0.4 fusion
  9.8 3.0 %collective-permute-start = (bf16[3,384,256]{2,1,0:T(8,128)(2,1)S(1)}, bf16[3,384,256]{2,1,0:T(8,128)(2,1)S(1)}, u32[]{:S(2)}, u32[]{:S(2)}) collective-permute-start(bf16[3,384,256]{2,1,0:T(8,128)(2,1)S(1)} %pad_maximum_fusion.1), channel_id=1, source_target_pairs={{0,16},{16,0},{1,17},{17,1},{2,18},{18,2},{3,19},{19,3},{4,20},{20... | collective-permute-start | bytes 1769480 | tf_op jit(solution)/shard_map/ppermute | solution.py:13
  12.9 13.3 %collective-permute-done = bf16[3,384,256]{2,1,0:T(8,128)(2,1)S(1)} collective-permute-done((bf16[3,384,256]{2,1,0:T(8,128)(2,1)S(1)}, bf16[3,384,256]{2,1,0:T(8,128)(2,1)S(1)}, u32[]{:S(2)}, u32[]{:S(2)}) %collective-permute-start) | collective-permute-done | bytes 589856 | tf_op jit(solution)/shard_map/ppermute | solution.py:13
  26.2 1.1 pad_maximum_fusion
  27.3 3.9 %fusion.14 = (bf16[384,1536]{1,0:T(8,128)(2,1)}, bf16[384,1536]{1,0:T(8,128)(2,1)}, bf16[384,1536]{1,0:T(8,128)(2,1)}) fusion(bf16[384,6144]{1,0:T(8,128)(2,1)} %bitcast.41), kind=kLoop, calls=%fused_computation.35 | loop fusion | bytes 7077888 | tf_op jit(solution)/shard_map/slice | solution.py:155
  31.2 1.7 collective-permute-start.5
  33.0 0.3 collective-permute-start.4
  33.3 1.7 collective-permute-start.3
  35.0 2.4 %fusion.15 = (bf16[384,768]{1,0:T(8,128)(2,1)}, bf16[384,768]{1,0:T(8,128)(2,1)}) fusion(bf16[384,6144]{1,0:T(8,128)(2,1)} %bitcast.42), kind=kLoop, calls=%fused_computation.36 | loop fusion | bytes 2359296 | tf_op jit(solution)/shard_map/slice | solution.py:155
  37.4 0.2 collective-permute-start.2
  37.6 1.8 %collective-permute-start.1 = (bf16[384,768]{1,0:T(8,128)(2,1)}, bf16[384,768]{1,0:T(8,128)(2,1)}, u32[]{:S(2)}, u32[]{:S(2)}) collective-permute-start(bf16[384,768]{1,0:T(8,128)(2,1)} %get-tuple-element.13), channel_id=1, source_target_pairs={{0,16},{16,0},{1,17},{17,1},{2,18},{18,2},{3,19},{19,3},{4,20},{20... | collective-permute-start | bytes 1769480 | tf_op jit(solution)/shard_map/ppermute | solution.py:13
  39.5 0.1 eq.32
  39.6 0.1 copy.16
  39.7 0.1 copy.17
  39.8 0.1 fusion.6
  40.0 0.1 copy.18
  40.1 0.1 reshape.92.table_ref
  40.3 0.4 fusion.1
  40.7 0.9 slice.30
  41.7 18.8 %collective-permute-done.5.other_ref = bf16[384,1536]{1,0:T(8,128)(2,1)} collective-permute-done((bf16[384,1536]{1,0:T(8,128)(2,1)}, bf16[384,1536]{1,0:T(8,128)(2,1)}, u32[]{:S(2)}, u32[]{:S(2)}) %collective-permute-start.5) | collective-permute-done | bytes 1179680 | tf_op jit(solution)/shard_map/ppermute | solution.py:13
  60.5 69.2 %all-gather.3.cloned.1.call-done = bf16[64,384,256]{2,1,0:T(8,128)(2,1)} async-done(((bf16[4,384,256]{2,1,0:T(8,128)(2,1)}), bf16[64,384,256]{2,1,0:T(8,128)(2,1)}) %all-gather.3.cloned.1.call-update) | async-done | bytes 12582928 | tf_op jit(solution)/shard_map/all_gather | solution.py:159
  129.7 3.7 %copy-done.1 = bf16[1,384,12288]{2,1,0:T(8,128)(2,1)S(1)} copy-done((bf16[1,384,12288]{2,1,0:T(8,128)(2,1)S(1)}, bf16[1,384,12288]{2,1,0:T(8,128)(2,1)}, u32[]{:S(2)}) %copy-start.1) | copy-done | bytes 9437208
  133.4 2.3 %copy-done.3 = bf16[1,384,6144]{2,1,0:T(8,128)(2,1)S(1)} copy-done((bf16[1,384,6144]{2,1,0:T(8,128)(2,1)S(1)}, bf16[1,384,6144]{2,1,0:T(8,128)(2,1)}, u32[]{:S(2)}) %copy-start.3) | copy-done | bytes 4718616
  135.7 7.0 %assemble.5.rest_0_ = bf16[384,12288]{1,0:T(8,128)(2,1)} custom-call(s32[192]{0:T(256)S(1)} %reshape.92.table_ref, s32[2]{0:T(128)S(1)} %pad_add_fusion.1.place_ref, bf16[3,384,256]{2,1,0:T(8,128)(2,1)S(1)} %pad_maximum_fusion.2.lefts_ref, bf16[16,4,384,256]{3,2,1,0:T(8,128)(2,1)} %bitcast.48, bf16[384,6144]{1,0:T(8,128)(2,1)S(1)} %bitcast.43, ...), custom_call_target="tpu_custom_call" | custom-call | tf_op jit(solution)/shard_map/assemble/pallas_call | solution.py:105
  142.7 3.7 %copy-done.2 = bf16[1,384,12288]{2,1,0:T(8,128)(2,1)S(1)} copy-done((bf16[1,384,12288]{2,1,0:T(8,128)(2,1)S(1)}, bf16[1,384,12288]{2,1,0:T(8,128)(2,1)}, u32[]{:S(2)}) %copy-start.2) | copy-done | bytes 9437208
  146.4 6.6 %assemble.6.rest_0_ = bf16[384,12288]{1,0:T(8,128)(2,1)} custom-call(s32[192]{0:T(256)S(1)} %reshape.92.table_ref, s32[2]{0:T(128)S(1)} %pad_add_fusion.1.place_ref, bf16[3,384,256]{2,1,0:T(8,128)(2,1)S(1)} %pad_maximum_fusion.2.lefts_ref, bf16[16,4,384,256]{3,2,1,0:T(8,128)(2,1)} %bitcast.49, ...), custom_call_target="tpu_custom_call", output_to_operand_aliasing={{}: (7, {})} | custom-call | tf_op jit(solution)/shard_map/assemble/pallas_call | solution.py:105
  152.9 6.6 %assemble.7.rest_0_ = bf16[384,12288]{1,0:T(8,128)(2,1)} custom-call(s32[192]{0:T(256)S(1)} %reshape.92.table_ref, s32[2]{0:T(128)S(1)} %pad_add_fusion.1.place_ref, bf16[3,384,256]{2,1,0:T(8,128)(2,1)S(1)} %pad_maximum_fusion.2.lefts_ref, bf16[16,4,384,256]{3,2,1,0:T(8,128)(2,1)} %bitcast.50, ...), custom_call_target="tpu_custom_call", output_to_operand_aliasing={{}: (7, {})} | custom-call | tf_op jit(solution)/shard_map/assemble/pallas_call | solution.py:105
  159.5 4.0 %assemble.8.rest_0_ = bf16[384,12288]{1,0:T(8,128)(2,1)} custom-call(s32[192]{0:T(256)S(1)} %reshape.92.table_ref, s32[2]{0:T(128)S(1)} %pad_add_fusion.1.place_ref, bf16[3,384,256]{2,1,0:T(8,128)(2,1)S(1)} %pad_maximum_fusion.2.lefts_ref, bf16[16,4,384,256]{3,2,1,0:T(8,128)(2,1)} %bitcast.51, ...), custom_call_target="tpu_custom_call", output_to_operand_aliasing={{}: (7, {})} | custom-call | tf_op jit(solution)/shard_map/assemble/pallas_call | solution.py:105
  163.5 4.0 %assemble.9 = bf16[384,12288]{1,0:T(8,128)(2,1)} custom-call(s32[192]{0:T(256)S(1)} %reshape.92.table_ref, s32[2]{0:T(128)S(1)} %pad_add_fusion.1.place_ref, bf16[3,384,256]{2,1,0:T(8,128)(2,1)S(1)} %pad_maximum_fusion.2.lefts_ref, bf16[16,4,384,256]{3,2,1,0:T(8,128)(2,1)} %bitcast.52, ...), custom_call_target="tpu_custom_call", output_to_operand_aliasing={{}: (7, {})} | custom-call | tf_op jit(solution)/shard_map/assemble/pallas_call | solution.py:105
  (29 shorter events, 0.6 us)
Async XLA Ops:
  6.5 2.8 %copy-start = (f32[1,256,256]{2,1,0:T(8,128)S(1)}, f32[1,256,256]{2,1,0:T(8,128)}, u32[]{:S(2)}) copy-start(f32[1,256,256]{2,1,0:T(8,128)} %param.10) | copy-start | bytes 786436
  6.5 123.2 %all-gather.3.cloned.1.call-start = ((), (), s32[]{:S(2)}) async-start(), calls=%async_computation | async-start | bytes 13369344 | tf_op jit(solution)/shard_map/all_gather | solution.py:159
  9.8 16.4 %collective-permute-start = (bf16[3,384,256]{2,1,0:T(8,128)(2,1)S(1)}, bf16[3,384,256]{2,1,0:T(8,128)(2,1)S(1)}, u32[]{:S(2)}, u32[]{:S(2)}) collective-permute-start(bf16[3,384,256]{2,1,0:T(8,128)(2,1)S(1)} %pad_maximum_fusion.1), channel_id=1, source_target_pairs={{0,16},{16,0},{1,17},{17,1},{2,18},{18,2},{3,19},{19,3},{4,20},{20... | collective-permute-start | bytes 1769480 | tf_op jit(solution)/shard_map/ppermute | solution.py:13
  26.2 7.1 %copy-start.4 = (bf16[3,384,256]{2,1,0:T(8,128)(2,1)}, bf16[3,384,256]{2,1,0:T(8,128)(2,1)S(1)}, u32[]{:S(2)}) copy-start(bf16[3,384,256]{2,1,0:T(8,128)(2,1)S(1)} %collective-permute-done) | copy-start | bytes 1769476
  27.3 12.2 %copy-start.6 = (s32[2,48]{1,0:T(2,128)S(1)}, s32[2,48]{1,0:T(2,128)}, u32[]{:S(2)}) copy-start(s32[2,48]{1,0:T(2,128)} %param.13) | copy-start | bytes 1156
  27.3 13.0 %copy-start.5 = (f32[1,256,256]{2,1,0:T(8,128)S(1)}, f32[1,256,256]{2,1,0:T(8,128)}, u32[]{:S(2)}) copy-start(f32[1,256,256]{2,1,0:T(8,128)} %param.15) | copy-start | bytes 786436
  31.2 29.2 %collective-permute-start.5 = (bf16[384,1536]{1,0:T(8,128)(2,1)}, bf16[384,1536]{1,0:T(8,128)(2,1)}, u32[]{:S(2)}, u32[]{:S(2)}) collective-permute-start(bf16[384,1536]{1,0:T(8,128)(2,1)} %get-tuple-element.9), channel_id=1, source_target_pairs={{0,16},{16,0},{1,17},{17,1},{2,18},{18,2},{3,19},{19,3},{4,20},{20... | collective-permute-start | bytes 3538952 | tf_op jit(solution)/shard_map/ppermute | solution.py:13
  33.0 109.7 %collective-permute-start.4 = (bf16[384,1536]{1,0:T(8,128)(2,1)}, bf16[384,1536]{1,0:T(8,128)(2,1)S(1)}, u32[]{:S(2)}, u32[]{:S(2)}) collective-permute-start(bf16[384,1536]{1,0:T(8,128)(2,1)} %get-tuple-element.10), channel_id=1, source_target_pairs={{0,16},{16,0},{1,17},{17,1},{2,18},{18,2},{3,19},{19,3},{4,20},{20... | collective-permute-start | bytes 3538952 | tf_op jit(solution)/shard_map/ppermute | solution.py:13
  33.3 119.7 %collective-permute-start.3 = (bf16[384,1536]{1,0:T(8,128)(2,1)}, bf16[384,1536]{1,0:T(8,128)(2,1)S(1)}, u32[]{:S(2)}, u32[]{:S(2)}) collective-permute-start(bf16[384,1536]{1,0:T(8,128)(2,1)} %get-tuple-element.11), channel_id=1, source_target_pairs={{0,16},{16,0},{1,17},{17,1},{2,18},{18,2},{3,19},{19,3},{4,20},{20... | collective-permute-start | bytes 3538952 | tf_op jit(solution)/shard_map/ppermute | solution.py:13
  37.4 122.1 %collective-permute-start.2 = (bf16[384,768]{1,0:T(8,128)(2,1)}, bf16[384,768]{1,0:T(8,128)(2,1)}, u32[]{:S(2)}, u32[]{:S(2)}) collective-permute-start(bf16[384,768]{1,0:T(8,128)(2,1)} %get-tuple-element.12), channel_id=1, source_target_pairs={{0,16},{16,0},{1,17},{17,1},{2,18},{18,2},{3,19},{19,3},{4,20},{20... | collective-permute-start | bytes 1769480 | tf_op jit(solution)/shard_map/ppermute | solution.py:13
  37.6 125.9 %collective-permute-start.1 = (bf16[384,768]{1,0:T(8,128)(2,1)}, bf16[384,768]{1,0:T(8,128)(2,1)}, u32[]{:S(2)}, u32[]{:S(2)}) collective-permute-start(bf16[384,768]{1,0:T(8,128)(2,1)} %get-tuple-element.13), channel_id=1, source_target_pairs={{0,16},{16,0},{1,17},{17,1},{2,18},{18,2},{3,19},{19,3},{4,20},{20... | collective-permute-start | bytes 1769480 | tf_op jit(solution)/shard_map/ppermute | solution.py:13
  129.7 3.7 %copy-start.1 = (bf16[1,384,12288]{2,1,0:T(8,128)(2,1)S(1)}, bf16[1,384,12288]{2,1,0:T(8,128)(2,1)}, u32[]{:S(2)}) copy-start(bf16[1,384,12288]{2,1,0:T(8,128)(2,1)} %param.16) | copy-start | bytes 28311556
  133.4 2.3 %copy-start.3 = (bf16[1,384,6144]{2,1,0:T(8,128)(2,1)S(1)}, bf16[1,384,6144]{2,1,0:T(8,128)(2,1)}, u32[]{:S(2)}) copy-start(bf16[1,384,6144]{2,1,0:T(8,128)(2,1)} %param.11) | copy-start | bytes 14155780
  142.7 3.7 %copy-start.2 = (bf16[1,384,12288]{2,1,0:T(8,128)(2,1)S(1)}, bf16[1,384,12288]{2,1,0:T(8,128)(2,1)}, u32[]{:S(2)}) copy-start(bf16[1,384,12288]{2,1,0:T(8,128)(2,1)} %param.16) | copy-start | bytes 28311556
Sparse Core Ops, SparseCore 0:
  27.4 102.2 all-gather.2

commit v2 on v1

v2 whole, which is shorter than its diff:
```python
import jax
import jax.numpy as jnp
from jax import lax
from jax.experimental import pallas as pl
from jax.experimental.pallas import tpu as pltpu
from jax.sharding import PartitionSpec as P

BLOCK = 128


def swap(array, axis, bit):
    return lax.ppermute(array, axis, [(i, i ^ 1 << bit) for i in range(lax.axis_size(axis))])


def shift(array, axis, by):
    extent = lax.axis_size(axis)
    return lax.ppermute(array, axis, [(i, (i + by) % extent) for i in range(extent)])


def masked_rows(panel, pattern_row, start):
    blocks = panel.shape[0] // BLOCK
    window = lax.dynamic_slice_in_dim(pattern_row, start, blocks)
    return panel * jnp.repeat(window, BLOCK).astype(panel.dtype)[:, None]


def left_factor(masked, inverse):
    return jnp.dot(masked.astype(jnp.float32), inverse, precision=lax.Precision.HIGHEST).astype(jnp.bfloat16)


def source_table(mapping, positions, parent_blocks):
    each = mapping.shape[0] // positions
    width = parent_blocks // (2 * positions)
    target = jnp.arange(parent_blocks, dtype=jnp.int32).reshape(2, positions, width)
    hit = mapping.reshape(1, positions, 1, each) == target[..., None]
    return jnp.sum(jnp.where(hit, jnp.arange(1, each + 1, dtype=jnp.int32), 0), axis=-1) - 1


def after(array, *earlier):
    return lax.optimization_barrier((array,) + earlier)[0]


def in_hbm(array):
    return pltpu.with_memory_space_constraint(array, pltpu.MemorySpace.HBM)


def assemble_group(at, positions, cols, each, width, table, place, lefts, own_set, other_set, own, other, trailing, previous):
    rows = own.shape[0]
    span = each * BLOCK
    wide = width * BLOCK
    row_blocks = rows // BLOCK
    zero = row_blocks * each

    def kernel(table_ref, place_ref, lefts_ref, own_set_ref, other_set_ref, own_ref, other_ref, trailing_ref, *rest):
        out_ref, schur_ref = rest[-2:]
        half = pl.program_id(0)
        own_half = place_ref[0]
        position = place_ref[1]

        def source(child, which_half, window, k):
            return table_ref[((child * 2 + which_half) * positions + window) * width + k]

        def panel_piece(child, j, which):
            if child == 0:
                return own_set_ref[j, which]
            return other_set_ref[(place_ref[3] + cols - j) % cols, which]

        @pl.when(half == 0)
        def _():
            for child, piece in enumerate((own_ref, other_ref)):
                for j in range(cols):
                    update = lax.dot_general(
                        lefts_ref[child], panel_piece(child, j, 0), (((1,), (1,)), ((), ())),
                        preferred_element_type=jnp.float32,
                    )
                    schur = (piece[:, j * span:(j + 1) * span].astype(jnp.float32) - update).astype(jnp.bfloat16)
                    for r in range(row_blocks):
                        for c in range(each):
                            schur_ref[child, j, r * each + c] = schur[r * BLOCK:(r + 1) * BLOCK, c * BLOCK:(c + 1) * BLOCK]
                    schur_ref[child, j, zero] = jnp.zeros((BLOCK, BLOCK), jnp.bfloat16)

        def emit(child_of_half):
            for j in range(cols):
                window = place_ref[2] + j
                update = lax.dot_general(
                    lefts_ref[2], panel_piece(child_of_half, j, 1), (((1,), (1,)), ((), ())),
                    preferred_element_type=jnp.float32,
                )
                base = trailing_ref[:, j * wide:(j + 1) * wide].astype(jnp.float32) - update
                for a in range(row_blocks):
                    for k in range(width):
                        blocks = []
                        for child in range(2):
                            r = source(child, own_half, position, a)
                            c = source(child, half, window, k)
                            which = jnp.where((r >= 0) & (c >= 0), r * each + c, zero)
                            blocks.append(schur_ref[child, j, which])
                        total = (blocks[0] + blocks[1]).astype(jnp.float32)
                        piece = base[a * BLOCK:(a + 1) * BLOCK, k * BLOCK:(k + 1) * BLOCK] + total
                        at_column = j * wide + k * BLOCK
                        out_ref[a * BLOCK:(a + 1) * BLOCK, at_column:at_column + BLOCK] = piece.astype(jnp.bfloat16)

        pl.when(half == own_half)(lambda: emit(0))
        pl.when(half != own_half)(lambda: emit(1))

    halves = positions // cols
    in_specs = [
        pl.BlockSpec(lefts.shape, lambda h, t, p: (0, 0, 0)),
        pl.BlockSpec((cols,) + own_set.shape[1:], lambda h, t, p: (p[2] // cols, 0, 0, 0)),
        pl.BlockSpec(other_set.shape, lambda h, t, p: (0, 0, 0, 0)),
        pl.BlockSpec((rows, cols * span), lambda h, t, p: (0, p[2] // cols)),
        pl.BlockSpec((rows, cols * span), lambda h, t, p: (0, at)),
        pl.BlockSpec((rows, cols * wide), lambda h, t, p: (0, h * halves + p[2] // cols)),
    ]
    operands = [lefts, in_hbm(own_set), in_hbm(other_set), in_hbm(own), in_hbm(other), in_hbm(trailing)]
    aliases = {}
    if previous is not None:
        in_specs.append(pl.BlockSpec(memory_space=pl.ANY))
        operands.append(previous)
        aliases = {len(operands) + 1: 0}
    windows = cols * rows
    return pl.pallas_call(
        kernel,
        grid_spec=pltpu.PrefetchScalarGridSpec(
            num_scalar_prefetch=2,
            grid=(2,),
            in_specs=in_specs,
            out_specs=pl.BlockSpec((rows, cols * wide), lambda h, t, p: (0, h * halves + p[2] // cols)),
            scratch_shapes=[pltpu.VMEM((2, cols, zero + 1, BLOCK, BLOCK), jnp.bfloat16)],
        ),
        out_shape=jax.ShapeDtypeStruct(trailing.shape, jnp.bfloat16),
        input_output_aliases=aliases,
        name="assemble",
        cost_estimate=pl.CostEstimate(
            flops=4 * windows * lefts.shape[2] * (span + wide),
            bytes_accessed=4 * windows * (span + 2 * wide) + 2 * (2 * other_set.size + lefts.size),
            transcendentals=0,
        ),
        compiler_params=pltpu.CompilerParams(vmem_limit_bytes=48 * 1024 * 1024),
    )(table, place, *operands)


def local(
    child_panel,
    child_inverse,
    child_trailing,
    child_pattern,
    child_map,
    parent_panel,
    parent_inverse,
    parent_trailing,
    parent_pattern,
):
    plane = ("row", "col")
    positions = lax.axis_size(plane)
    cols = lax.axis_size("col")
    row = lax.axis_index("row")
    col = lax.axis_index("col")
    position = lax.axis_index(plane)
    cube_index = lax.axis_index("cube")
    half_bit = cube_index % 2
    parent = cube_index // 2
    parent_blocks = parent_pattern.shape[1]
    each = child_map.shape[1] // positions
    width = parent_blocks // (2 * positions)
    own = child_trailing[0]
    trailing = parent_trailing[0]
    rows = own.shape[0]
    span = each * BLOCK

    own_child = masked_rows(child_panel[0], child_pattern[0], position * each)
    pattern_row = lax.dynamic_index_in_dim(parent_pattern, parent, 0, keepdims=False)
    own_parent = masked_rows(parent_panel[0], pattern_row, half_bit * (parent_blocks // 2) + position * width)
    own_piece = jnp.stack([own_child, own_parent])
    other_piece = swap(own_piece, "cube", 0)

    child_left = left_factor(own_child, child_inverse[0])
    parent_left = left_factor(own_parent, lax.dynamic_index_in_dim(parent_inverse, parent, 0, keepdims=False))
    other_left = swap(child_left, "cube", 0)
    lefts = jnp.stack([child_left, other_left, parent_left])

    def own_columns(deltas):
        parts = [lax.dynamic_slice_in_dim(own, (row ^ delta) * cols * span, cols * span, 1) for delta in deltas]
        return parts[0] if len(parts) == 1 else jnp.concatenate(parts, axis=1)

    own_set = lax.all_gather(own_piece, plane, axis=0, tiled=False)

    early = swap(after(own_columns([0, 1, 2]), other_piece), "cube", 0)
    late = swap(own_columns([3]), "cube", 0)

    shifted = [shift(other_piece, "col", j) for j in range(1, cols)]
    across = [swap(other_piece, "row", 1)]
    across.append(swap(after(shifted[0], across[0]), "row", 1))
    across.append(swap(shifted[1], "row", 1))
    across.append(swap(after(shifted[2], across[1]), "row", 1))
    near = jnp.stack([other_piece] + shifted)
    far = jnp.stack(across)
    other_sets = [near, swap(near, "row", 0), far, swap(after(far, early), "row", 0)]

    own_map = lax.dynamic_index_in_dim(child_map, cube_index, 0, keepdims=False)
    other_map = lax.dynamic_index_in_dim(child_map, cube_index ^ 1, 0, keepdims=False)
    table = jnp.stack([source_table(m, positions, parent_blocks) for m in (own_map, other_map)]).reshape(-1)

    result = None
    for delta, (other, at) in enumerate(((early, 0), (early, 1), (early, 2), (late, 0))):
        place = jnp.stack([half_bit, position, (row ^ delta) * cols, col]).astype(jnp.int32)
        result = assemble_group(
            at, positions, cols, each, width, table, place, lefts,
            own_set, other_sets[delta], own, other, trailing, result,
        )
    return result[None]


def solution(mesh):
    in_specs = (
        P("cube", ("row", "col"), None),
        P("cube", None, None),
        P("cube", ("row", "col"), None),
        P("cube", None),
        P(),
        P("cube", ("row", "col"), None),
        P(),
        P("cube", ("row", "col"), None),
        P(),
    )
    out_specs = P("cube", ("row", "col"), None)
    return jax.shard_map(local, mesh=mesh, in_specs=in_specs, out_specs=out_specs, check_vma=False)
```

time: 175 us -> 146 us (0.83)
  waiting for transfers between devices: 101 us -> 66.7 us
  local copies, waits for them, and re-layouts: 17.8 us -> 5.09 us
  starting transfers between devices: 8.83 us -> 18.4 us
  other arithmetic: 4.07 us -> 11.4 us
    all_gather x1, waiting for transfers between devices: 69.2 us -> 0.29 us  [local(): own_set = lax.all_gather(own_piece, plane, axis=0, tiled=False)]
    ppermute x6 -> x13, waiting for transfers between devices: 32.1 us -> 66.4 us  [the longest x10 35.9 us: swap(): lax.ppermute(array, axis, [(i, i ^ 1 << bit) for i in range(lax.axis_size...]
    ppermute x6 -> x13, starting transfers between devices: 8.82 us -> 18.4 us  [the longest x10 12.8 us: swap(): lax.ppermute(array, axis, [(i, i ^ 1 << bit) for i in range(lax.axis_size...]
    unnamed x14 -> x8, local copies, waits for them, and re-layouts: 9.71 us -> 0.69 us
    slice x4 -> x0, local copies, waits for them, and re-layouts: 7.31 us -> none  [the longest x2 6.35 us: local(): others.append(swap_cube(own[:, first * span:(first + size) * span]))]
    another operation x3 -> x6, other arithmetic: 0.21 us -> 5.85 us  [the longest x1 2.6 us: local(): far = jnp.stack(across)]
    dynamic_slice x0 -> x1, local copies, waits for them, and re-layouts: none -> 3.66 us  [own_columns(): lax.dynamic_slice_in_dim(own, (row ^ delta) * cols * span, cols * span, 1)]
    pallas_call x5 -> x4, Pallas kernels: 28.2 us -> 28.1 us  [assemble_group(): pl.pallas_call(kernel, grid_spec=pltpu.PrefetchScalarGridSpec(num_scalar_...]
  transfers between devices with their start and end apart: 7 -> 14, of which waited for: 3 -> 9; matrix products, arithmetic and copies ran while one was open for 5% -> 9% of each run, Pallas kernels for 14% -> 15%
where the time goes in v2:
time: 146 us; the launch traced here: 145 us
  waiting for transfers between devices  66.7 us (46%)
  Pallas kernels  28.1 us (19%)
  starting transfers between devices  18.4 us (13%)
  between operations  13.5 us (9%)
  other arithmetic  11.4 us (8%)
  local copies, waits for them, and re-layouts  5.09 us (3%)
  matrix products  1.66 us (1%)
    ppermute x10, waiting for transfers between devices, swap(): lax.ppermute(array, axis, [(i, i ^ 1 << bit) for i in range(lax.axis_size...  35.9 us
    ppermute x3, waiting for transfers between devices, shift(): lax.ppermute(array, axis, [(i, (i + by) % extent) for i in range(extent)])  30.5 us
    pallas_call x4, Pallas kernels, assemble_group(): pl.pallas_call(kernel, grid_spec=pltpu.PrefetchScalarGridSpec(num_scalar_...  28.1 us
    ppermute x10, starting transfers between devices, swap(): lax.ppermute(array, axis, [(i, i ^ 1 << bit) for i in range(lax.axis_size...  12.8 us
    ppermute x3, starting transfers between devices, shift(): lax.ppermute(array, axis, [(i, (i + by) % extent) for i in range(extent)])  5.51 us
    dynamic_slice x1, local copies, waits for them, and re-layouts, own_columns(): lax.dynamic_slice_in_dim(own, (row ^ delta) * cols * span, cols * span, 1)  3.66 us
  transfers between devices with their start and end apart: 14, of which 9 were waited for; matrix products, arithmetic and copies ran while one was open for 9% of the time, Pallas kernels for 15%

profile of v2, /device:TPU:0, one launch (start us, length us, event | category | flops | bytes accessed | tf_op | source)
XLA Modules:
  0.0 144.8 jit_solution(13148430044684740689)
XLA Ops:
  6.5 0.8 fusion.12
  7.4 0.7 fusion.10
  8.2 1.0 broadcast_multiply_fusion
  9.2 1.0 broadcast_multiply_fusion.1
  10.3 0.8 pad_maximum_fusion.4
  11.1 3.0 %collective-permute-start.1 = (bf16[2,384,256]{2,1,0:T(8,128)(2,1)}, bf16[2,384,256]{2,1,0:T(8,128)(2,1)S(1)}, u32[]{:S(2)}, u32[]{:S(2)}) collective-permute-start(bf16[2,384,256]{2,1,0:T(8,128)(2,1)} %pad_maximum_fusion.4), channel_id=1, source_target_pairs={{0,16},{16,0},{1,17},{17,1},{2,18},{18,2},{3,19},{19,3},{4,20},{20... | collective-permute-start | bytes 1179656 | tf_op jit(solution)/shard_map/ppermute | solution.py:12
  14.1 3.7 %dynamic-slice_bitcast_fusion = (bf16[384,1536]{1,0:T(8,128)(2,1)}, bf16[384,1536]{1,0:T(8,128)(2,1)S(1)}, bf16[384,1536]{1,0:T(8,128)(2,1)S(1)}, bf16[384,1536]{1,0:T(8,128)(2,1)S(1)}) fusion(bf16[1,384,6144]{2,1,0:T(8,128)(2,1)} %param.11, s32[]{:T(128)S(6)} %select_n.55, s32[]{:T(128)S(6)} %select_n.54, s32[]{:T(128)S(6)} %select_n.53, s32[]{:T(128)S(6)} %select_n.52), kind=kLoop, calls=%fused_computation.3 | loop fusion | bytes 9437200 | tf_op jit(solution)/shard_map/dynamic_slice | solution.py:182
  17.8 1.9 %pad_maximum_fusion = bf16[384,4608]{1,0:T(8,128)(2,1)} fusion(bf16[384,1536]{1,0:T(8,128)(2,1)S(1)} %get-tuple-element.20, bf16[384,1536]{1,0:T(8,128)(2,1)S(1)} %get-tuple-element.21, bf16[384,1536]{1,0:T(8,128)(2,1)S(1)} %get-tuple-element.22), kind=kLoop, calls=%fused_computation | loop fusion | flops 10616832 | bytes 7077888 | tf_op jit(solution)/shard_map/concatenate | solution.py:183
  19.7 3.8 %collective-permute-done.1 = bf16[2,384,256]{2,1,0:T(8,128)(2,1)S(1)} collective-permute-done((bf16[2,384,256]{2,1,0:T(8,128)(2,1)}, bf16[2,384,256]{2,1,0:T(8,128)(2,1)S(1)}, u32[]{:S(2)}, u32[]{:S(2)}) %collective-permute-start.1) | collective-permute-done | bytes 393248 | tf_op jit(solution)/shard_map/ppermute | solution.py:12
  23.4 1.7 %collective-permute-start.9 = (bf16[384,4608]{1,0:T(8,128)(2,1)}, bf16[384,4608]{1,0:T(8,128)(2,1)}, u32[]{:S(2)}, u32[]{:S(2)}) collective-permute-start(bf16[384,4608]{1,0:T(8,128)(2,1)} %pad_maximum_fusion), channel_id=1, source_target_pairs={{0,16},{16,0},{1,17},{17,1},{2,18},{18,2},{3,19},{19,3},{4,20},{20... | collective-permute-start | bytes 10616840 | tf_op jit(solution)/shard_map/ppermute | solution.py:12
  25.2 1.6 %collective-permute-start.3 = (bf16[2,384,256]{2,1,0:T(8,128)(2,1)S(1)}, bf16[2,384,256]{2,1,0:T(8,128)(2,1)S(1)}, u32[]{:S(2)}, u32[]{:S(2)}) collective-permute-start(bf16[2,384,256]{2,1,0:T(8,128)(2,1)S(1)} %collective-permute-done.1), channel_id=1, source_target_pairs={{0,1},{1,2},{2,3},{3,0},{4,5},{5,6},{6,7},{7,4},{8,9},{9,10},{10,1... | collective-permute-start | bytes 1179656 | tf_op jit(solution)/shard_map/ppermute | solution.py:17
  26.8 1.5 %collective-permute-start.2 = (bf16[2,384,256]{2,1,0:T(8,128)(2,1)S(1)}, bf16[2,384,256]{2,1,0:T(8,128)(2,1)S(1)}, u32[]{:S(2)}, u32[]{:S(2)}) collective-permute-start(bf16[2,384,256]{2,1,0:T(8,128)(2,1)S(1)} %collective-permute-done.1), channel_id=1, source_target_pairs={{0,8},{4,12},{8,0},{12,4},{1,9},{5,13},{9,1},{13,5},{2,10},{6,14},... | collective-permute-start | bytes 1179656 | tf_op jit(solution)/shard_map/ppermute | solution.py:12
  28.3 2.6 %collective-permute-start.5 = (bf16[2,384,256]{2,1,0:T(8,128)(2,1)S(1)}, bf16[2,384,256]{2,1,0:T(8,128)(2,1)}, u32[]{:S(2)}, u32[]{:S(2)}) collective-permute-start(bf16[2,384,256]{2,1,0:T(8,128)(2,1)S(1)} %collective-permute-done.1), channel_id=1, source_target_pairs={{0,2},{1,3},{2,0},{3,1},{4,6},{5,7},{6,4},{7,5},{8,10},{9,11},{10,... | collective-permute-start | bytes 1179656 | tf_op jit(solution)/shard_map/ppermute | solution.py:17
  30.8 1.3 collective-permute-start.7
  32.2 15.2 %collective-permute-done.3 = bf16[2,384,256]{2,1,0:T(8,128)(2,1)S(1)} collective-permute-done((bf16[2,384,256]{2,1,0:T(8,128)(2,1)S(1)}, bf16[2,384,256]{2,1,0:T(8,128)(2,1)S(1)}, u32[]{:S(2)}, u32[]{:S(2)}) %collective-permute-start.3) | collective-permute-done | bytes 393248 | tf_op jit(solution)/shard_map/ppermute | solution.py:17
  47.4 1.5 %collective-permute-start.4 = (bf16[2,384,256]{2,1,0:T(8,128)(2,1)S(1)}, bf16[2,384,256]{2,1,0:T(8,128)(2,1)S(1)}, u32[]{:S(2)}, u32[]{:S(2)}) collective-permute-start(bf16[2,384,256]{2,1,0:T(8,128)(2,1)S(1)} %collective-permute-done.3), channel_id=1, source_target_pairs={{0,8},{4,12},{8,0},{12,4},{1,9},{5,13},{9,1},{13,5},{2,10},{6,14},... | collective-permute-start | bytes 1179656 | tf_op jit(solution)/shard_map/ppermute | solution.py:12
  48.9 15.4 %collective-permute-done.5 = bf16[2,384,256]{2,1,0:T(8,128)(2,1)} collective-permute-done((bf16[2,384,256]{2,1,0:T(8,128)(2,1)S(1)}, bf16[2,384,256]{2,1,0:T(8,128)(2,1)}, u32[]{:S(2)}, u32[]{:S(2)}) %collective-permute-start.5) | collective-permute-done | bytes 393248 | tf_op jit(solution)/shard_map/ppermute | solution.py:17
  64.2 1.5 %collective-permute-start.6 = (bf16[2,384,256]{2,1,0:T(8,128)(2,1)}, bf16[2,384,256]{2,1,0:T(8,128)(2,1)}, u32[]{:S(2)}, u32[]{:S(2)}) collective-permute-start(bf16[2,384,256]{2,1,0:T(8,128)(2,1)} %collective-permute-done.5), channel_id=1, source_target_pairs={{0,8},{4,12},{8,0},{12,4},{1,9},{5,13},{9,1},{13,5},{2,10},{6,14},... | collective-permute-start | bytes 1179656 | tf_op jit(solution)/shard_map/ppermute | solution.py:12
  66.2 1.3 pad_maximum_fusion.2.other_set_ref
  68.0 1.5 %collective-permute-start = (bf16[384,256]{1,0:T(8,128)(2,1)S(1)}, bf16[384,256]{1,0:T(8,128)(2,1)S(1)}, u32[]{:S(2)}, u32[]{:S(2)}) collective-permute-start(bf16[384,256]{1,0:T(8,128)(2,1)S(1)} %convolution_convert_fusion.1), channel_id=1, source_target_pairs={{0,16},{16,0},{1,17},{17,1},{2,18},{18,2},{3,19},{19,3},{4,20},{20... | collective-permute-start | bytes 589832 | tf_op jit(solution)/shard_map/ppermute | solution.py:12
  69.9 14.7 %collective-permute-done.6 = bf16[2,384,256]{2,1,0:T(8,128)(2,1)} collective-permute-done((bf16[2,384,256]{2,1,0:T(8,128)(2,1)}, bf16[2,384,256]{2,1,0:T(8,128)(2,1)}, u32[]{:S(2)}, u32[]{:S(2)}) %collective-permute-start.6) | collective-permute-done | bytes 393248 | tf_op jit(solution)/shard_map/ppermute | solution.py:12
  84.7 1.5 %collective-permute-start.11 = (bf16[384,1536]{1,0:T(8,128)(2,1)}, bf16[384,1536]{1,0:T(8,128)(2,1)}, u32[]{:S(2)}, u32[]{:S(2)}) collective-permute-start(bf16[384,1536]{1,0:T(8,128)(2,1)} %get-tuple-element.19), channel_id=1, source_target_pairs={{0,16},{16,0},{1,17},{17,1},{2,18},{18,2},{3,19},{19,3},{4,20},{20... | collective-permute-start | bytes 3538952 | tf_op jit(solution)/shard_map/ppermute | solution.py:12
  86.1 14.2 %collective-permute-done.8 = bf16[2,384,256]{2,1,0:T(8,128)(2,1)} collective-permute-done((bf16[2,384,256]{2,1,0:T(8,128)(2,1)}, bf16[2,384,256]{2,1,0:T(8,128)(2,1)}, u32[]{:S(2)}, u32[]{:S(2)}) %collective-permute-start.8) | collective-permute-done | bytes 393248 | tf_op jit(solution)/shard_map/ppermute | solution.py:12
  100.3 2.6 %pad_maximum_fusion.1.other_set_ref = bf16[4,2,384,256]{3,2,1,0:T(8,128)(2,1)} fusion(bf16[1,2,384,256]{3,2,1,0:T(8,128)(2,1)} %bitcast.21, bf16[1,2,384,256]{3,2,1,0:T(8,128)(2,1)} %bitcast.20, bf16[1,2,384,256]{3,2,1,0:T(8,128)(2,1)S(1)} %bitcast.72, bf16[1,2,384,256]{3,2,1,0:T(8,128)(2,1)S(1)} %bitcast.71), kind=kLoop, calls=%fused_computation.1 | loop fusion | flops 2359296 | bytes 3145728 | tf_op jit(solution)/shard_map/stack | solution.py:196
  103.7 1.3 fusion
  105.1 2.3 %collective-permute-done = bf16[384,256]{1,0:T(8,128)(2,1)S(1)} collective-permute-done((bf16[384,256]{1,0:T(8,128)(2,1)S(1)}, bf16[384,256]{1,0:T(8,128)(2,1)S(1)}, u32[]{:S(2)}, u32[]{:S(2)}) %collective-permute-start) | collective-permute-done | bytes 196640 | tf_op jit(solution)/shard_map/ppermute | solution.py:12
  107.3 0.7 copy-done.2
  108.0 1.0 pad_maximum_fusion.3.lefts_ref
  109.3 7.0 %assemble.4.rest_0_ = bf16[384,12288]{1,0:T(8,128)(2,1)} custom-call(s32[192]{0:T(256)S(1)} %reshape.96.table_ref, s32[4]{0:T(128)S(1)} %get-tuple-element.17.place_ref, bf16[3,384,256]{2,1,0:T(8,128)(2,1)S(1)} %pad_maximum_fusion.3.lefts_ref, bf16[16,2,384,256]{3,2,1,0:T(8,128)(2,1)} %bitcast.65, bf16[4,2,384,256]{3,2,1,0:T(8,128)(2,1)} %copy-done.1, ...), custom_call_target="tpu_custom_call" | custom-call | flops 1207959552 | bytes 10813440 | tf_op jit(solution)/shard_map/assemble/pallas_call | solution.py:121
  116.3 7.0 %assemble.5.rest_0_ = bf16[384,12288]{1,0:T(8,128)(2,1)} custom-call(s32[192]{0:T(256)S(1)} %reshape.96.table_ref, s32[4]{0:T(128)S(1)} %get-tuple-element.23.place_ref, bf16[3,384,256]{2,1,0:T(8,128)(2,1)S(1)} %pad_maximum_fusion.3.lefts_ref, bf16[16,2,384,256]{3,2,1,0:T(8,128)(2,1)} %bitcast.66, ...), custom_call_target="tpu_custom_call", output_to_operand_aliasing={{}: (8, {})} | custom-call | flops 1207959552 | bytes 10813440 | tf_op jit(solution)/shard_map/assemble/pallas_call | solution.py:121
  123.4 7.0 %assemble.6.rest_0_ = bf16[384,12288]{1,0:T(8,128)(2,1)} custom-call(s32[192]{0:T(256)S(1)} %reshape.96.table_ref, s32[4]{0:T(128)S(1)} %get-tuple-element.24.place_ref, bf16[3,384,256]{2,1,0:T(8,128)(2,1)S(1)} %pad_maximum_fusion.3.lefts_ref, bf16[16,2,384,256]{3,2,1,0:T(8,128)(2,1)} %bitcast.67, ...), custom_call_target="tpu_custom_call", output_to_operand_aliasing={{}: (8, {})} | custom-call | flops 1207959552 | bytes 10813440 | tf_op jit(solution)/shard_map/assemble/pallas_call | solution.py:121
  131.0 7.0 %assemble.7 = bf16[384,12288]{1,0:T(8,128)(2,1)} custom-call(s32[192]{0:T(256)S(1)} %reshape.96.table_ref, s32[4]{0:T(128)S(1)} %get-tuple-element.25.place_ref, bf16[3,384,256]{2,1,0:T(8,128)(2,1)S(1)} %pad_maximum_fusion.3.lefts_ref, bf16[16,2,384,256]{3,2,1,0:T(8,128)(2,1)} %bitcast.68, ...), custom_call_target="tpu_custom_call", output_to_operand_aliasing={{}: (8, {})} | custom-call | flops 1207959552 | bytes 10813440 | tf_op jit(solution)/shard_map/assemble/pallas_call | solution.py:121
  (37 shorter events, 3.2 us)
Async XLA Ops:
  6.5 61.1 %copy-start = (f32[1,256,256]{2,1,0:T(8,128)S(1)}, f32[1,256,256]{2,1,0:T(8,128)}, u32[]{:S(2)}) copy-start(f32[1,256,256]{2,1,0:T(8,128)} %param.10) | copy-start | bytes 786436
  6.5 102.8 %all-gather.3.cloned.1.call-start = ((), (), s32[]{:S(2)}) async-start(), calls=%async_computation | async-start | bytes 6684672 | tf_op jit(solution)/shard_map/all_gather | solution.py:185
  11.1 12.4 %collective-permute-start.1 = (bf16[2,384,256]{2,1,0:T(8,128)(2,1)}, bf16[2,384,256]{2,1,0:T(8,128)(2,1)S(1)}, u32[]{:S(2)}, u32[]{:S(2)}) collective-permute-start(bf16[2,384,256]{2,1,0:T(8,128)(2,1)} %pad_maximum_fusion.4), channel_id=1, source_target_pairs={{0,16},{16,0},{1,17},{17,1},{2,18},{18,2},{3,19},{19,3},{4,20},{20... | collective-permute-start | bytes 1179656 | tf_op jit(solution)/shard_map/ppermute | solution.py:12
  23.4 79.8 %collective-permute-start.9 = (bf16[384,4608]{1,0:T(8,128)(2,1)}, bf16[384,4608]{1,0:T(8,128)(2,1)}, u32[]{:S(2)}, u32[]{:S(2)}) collective-permute-start(bf16[384,4608]{1,0:T(8,128)(2,1)} %pad_maximum_fusion), channel_id=1, source_target_pairs={{0,16},{16,0},{1,17},{17,1},{2,18},{18,2},{3,19},{19,3},{4,20},{20... | collective-permute-start | bytes 10616840 | tf_op jit(solution)/shard_map/ppermute | solution.py:12
  25.2 22.2 %collective-permute-start.3 = (bf16[2,384,256]{2,1,0:T(8,128)(2,1)S(1)}, bf16[2,384,256]{2,1,0:T(8,128)(2,1)S(1)}, u32[]{:S(2)}, u32[]{:S(2)}) collective-permute-start(bf16[2,384,256]{2,1,0:T(8,128)(2,1)S(1)} %collective-permute-done.1), channel_id=1, source_target_pairs={{0,1},{1,2},{2,3},{3,0},{4,5},{5,6},{6,7},{7,4},{8,9},{9,10},{10,1... | collective-permute-start | bytes 1179656 | tf_op jit(solution)/shard_map/ppermute | solution.py:17
  26.8 20.6 %collective-permute-start.2 = (bf16[2,384,256]{2,1,0:T(8,128)(2,1)S(1)}, bf16[2,384,256]{2,1,0:T(8,128)(2,1)S(1)}, u32[]{:S(2)}, u32[]{:S(2)}) collective-permute-start(bf16[2,384,256]{2,1,0:T(8,128)(2,1)S(1)} %collective-permute-done.1), channel_id=1, source_target_pairs={{0,8},{4,12},{8,0},{12,4},{1,9},{5,13},{9,1},{13,5},{2,10},{6,14},... | collective-permute-start | bytes 1179656 | tf_op jit(solution)/shard_map/ppermute | solution.py:12
  28.3 35.9 %collective-permute-start.5 = (bf16[2,384,256]{2,1,0:T(8,128)(2,1)S(1)}, bf16[2,384,256]{2,1,0:T(8,128)(2,1)}, u32[]{:S(2)}, u32[]{:S(2)}) collective-permute-start(bf16[2,384,256]{2,1,0:T(8,128)(2,1)S(1)} %collective-permute-done.1), channel_id=1, source_target_pairs={{0,2},{1,3},{2,0},{3,1},{4,6},{5,7},{6,4},{7,5},{8,10},{9,11},{10,... | collective-permute-start | bytes 1179656 | tf_op jit(solution)/shard_map/ppermute | solution.py:17
  30.8 34.8 %collective-permute-start.7 = (bf16[2,384,256]{2,1,0:T(8,128)(2,1)S(1)}, bf16[2,384,256]{2,1,0:T(8,128)(2,1)}, u32[]{:S(2)}, u32[]{:S(2)}) collective-permute-start(bf16[2,384,256]{2,1,0:T(8,128)(2,1)S(1)} %collective-permute-done.1), channel_id=1, source_target_pairs={{0,3},{1,0},{2,1},{3,2},{4,7},{5,4},{6,5},{7,6},{8,11},{9,8},{10,9... | collective-permute-start | bytes 1179656 | tf_op jit(solution)/shard_map/ppermute | solution.py:17
  47.4 18.3 %collective-permute-start.4 = (bf16[2,384,256]{2,1,0:T(8,128)(2,1)S(1)}, bf16[2,384,256]{2,1,0:T(8,128)(2,1)S(1)}, u32[]{:S(2)}, u32[]{:S(2)}) collective-permute-start(bf16[2,384,256]{2,1,0:T(8,128)(2,1)S(1)} %collective-permute-done.3), channel_id=1, source_target_pairs={{0,8},{4,12},{8,0},{12,4},{1,9},{5,13},{9,1},{13,5},{2,10},{6,14},... | collective-permute-start | bytes 1179656 | tf_op jit(solution)/shard_map/ppermute | solution.py:12
  64.2 20.4 %collective-permute-start.6 = (bf16[2,384,256]{2,1,0:T(8,128)(2,1)}, bf16[2,384,256]{2,1,0:T(8,128)(2,1)}, u32[]{:S(2)}, u32[]{:S(2)}) collective-permute-start(bf16[2,384,256]{2,1,0:T(8,128)(2,1)} %collective-permute-done.5), channel_id=1, source_target_pairs={{0,8},{4,12},{8,0},{12,4},{1,9},{5,13},{9,1},{13,5},{2,10},{6,14},... | collective-permute-start | bytes 1179656 | tf_op jit(solution)/shard_map/ppermute | solution.py:12
  65.7 34.7 %collective-permute-start.8 = (bf16[2,384,256]{2,1,0:T(8,128)(2,1)}, bf16[2,384,256]{2,1,0:T(8,128)(2,1)}, u32[]{:S(2)}, u32[]{:S(2)}) collective-permute-start(bf16[2,384,256]{2,1,0:T(8,128)(2,1)} %collective-permute-done.7), channel_id=1, source_target_pairs={{0,8},{4,12},{8,0},{12,4},{1,9},{5,13},{9,1},{13,5},{2,10},{6,14},... | collective-permute-start | bytes 1179656 | tf_op jit(solution)/shard_map/ppermute | solution.py:12
  66.2 3.3 %copy-start.3 = (s32[2,48]{1,0:T(2,128)S(1)}, s32[2,48]{1,0:T(2,128)}, u32[]{:S(2)}) copy-start(s32[2,48]{1,0:T(2,128)} %param.13) | copy-start | bytes 1156
  67.6 35.4 %copy-start.1 = (bf16[4,2,384,256]{3,2,1,0:T(8,128)(2,1)}, bf16[4,2,384,256]{3,2,1,0:T(8,128)(2,1)S(1)}, u32[]{:S(2)}) copy-start(bf16[4,2,384,256]{3,2,1,0:T(8,128)(2,1)S(1)} %pad_maximum_fusion.2.other_set_ref) | copy-start | bytes 4718596
  67.6 48.8 %collective-permute-start.12 = (bf16[4,2,384,256]{3,2,1,0:T(8,128)(2,1)S(1)}, bf16[4,2,384,256]{3,2,1,0:T(8,128)(2,1)}, u32[]{:S(2)}, u32[]{:S(2)}) collective-permute-start(bf16[4,2,384,256]{3,2,1,0:T(8,128)(2,1)S(1)} %pad_maximum_fusion.2.other_set_ref), channel_id=1, source_target_pairs={{0,4},{4,0},{8,12},{12,8},{1,5},{5,1},{9,13},{13,9},{2,6},{6,2},{1... | collective-permute-start | bytes 4718600 | tf_op jit(solution)/shard_map/ppermute | solution.py:12
  68.0 39.3 %collective-permute-start = (bf16[384,256]{1,0:T(8,128)(2,1)S(1)}, bf16[384,256]{1,0:T(8,128)(2,1)S(1)}, u32[]{:S(2)}, u32[]{:S(2)}) collective-permute-start(bf16[384,256]{1,0:T(8,128)(2,1)S(1)} %convolution_convert_fusion.1), channel_id=1, source_target_pairs={{0,16},{16,0},{1,17},{17,1},{2,18},{18,2},{3,19},{19,3},{4,20},{20... | collective-permute-start | bytes 589832 | tf_op jit(solution)/shard_map/ppermute | solution.py:12
  84.7 46.3 %collective-permute-start.11 = (bf16[384,1536]{1,0:T(8,128)(2,1)}, bf16[384,1536]{1,0:T(8,128)(2,1)}, u32[]{:S(2)}, u32[]{:S(2)}) collective-permute-start(bf16[384,1536]{1,0:T(8,128)(2,1)} %get-tuple-element.19), channel_id=1, source_target_pairs={{0,16},{16,0},{1,17},{17,1},{2,18},{18,2},{3,19},{19,3},{4,20},{20... | collective-permute-start | bytes 3538952 | tf_op jit(solution)/shard_map/ppermute | solution.py:12
  103.2 27.7 %collective-permute-start.10 = (bf16[4,2,384,256]{3,2,1,0:T(8,128)(2,1)}, bf16[4,2,384,256]{3,2,1,0:T(8,128)(2,1)}, u32[]{:S(2)}, u32[]{:S(2)}) collective-permute-start(bf16[4,2,384,256]{3,2,1,0:T(8,128)(2,1)} %pad_maximum_fusion.1.other_set_ref), channel_id=1, source_target_pairs={{0,4},{4,0},{8,12},{12,8},{1,5},{5,1},{9,13},{13,9},{2,6},{6,2},{1... | collective-permute-start | bytes 4718600 | tf_op jit(solution)/shard_map/ppermute | solution.py:12
  107.3 0.7 copy-start.2
Sparse Core Ops, SparseCore 0:
  11.2 98.0 all-gather.2

commit v3 on v2

--- a/solution.py
+++ b/solution.py
@@ -35,6 +35,14 @@
     return jnp.sum(jnp.where(hit, jnp.arange(1, each + 1, dtype=jnp.int32), 0), axis=-1) - 1
 
 
+def ring(piece):
+    extent = lax.axis_size("col")
+    held = [piece]
+    for _ in range(extent - 2):
+        held.append(shift(held[-1], "col", 1))
+    return held + [shift(piece, "col", extent - 1)]
+
+
 def after(array, *earlier):
     return lax.optimization_barrier((array,) + earlier)[0]
 
@@ -60,9 +68,8 @@
             return table_ref[((child * 2 + which_half) * positions + window) * width + k]
 
         def panel_piece(child, j, which):
-            if child == 0:
-                return own_set_ref[j, which]
-            return other_set_ref[(place_ref[3] + cols - j) % cols, which]
+            held = own_set_ref if child == 0 else other_set_ref
+            return held[(place_ref[3] + cols - j) % cols, which]
 
         @pl.when(half == 0)
         def _():
@@ -105,7 +112,7 @@
     halves = positions // cols
     in_specs = [
         pl.BlockSpec(lefts.shape, lambda h, t, p: (0, 0, 0)),
-        pl.BlockSpec((cols,) + own_set.shape[1:], lambda h, t, p: (p[2] // cols, 0, 0, 0)),
+        pl.BlockSpec(own_set.shape, lambda h, t, p: (0, 0, 0, 0)),
         pl.BlockSpec(other_set.shape, lambda h, t, p: (0, 0, 0, 0)),
         pl.BlockSpec((rows, cols * span), lambda h, t, p: (0, p[2] // cols)),
         pl.BlockSpec((rows, cols * span), lambda h, t, p: (0, at)),
@@ -182,19 +189,22 @@
         parts = [lax.dynamic_slice_in_dim(own, (row ^ delta) * cols * span, cols * span, 1) for delta in deltas]
         return parts[0] if len(parts) == 1 else jnp.concatenate(parts, axis=1)
 
-    own_set = lax.all_gather(own_piece, plane, axis=0, tiled=False)
-
-    early = swap(after(own_columns([0, 1, 2]), other_piece), "cube", 0)
+    early = swap(after(own_columns([0, 1, 2]), other_piece, other_left), "cube", 0)
     late = swap(own_columns([3]), "cube", 0)
 
-    shifted = [shift(other_piece, "col", j) for j in range(1, cols)]
-    across = [swap(other_piece, "row", 1)]
-    across.append(swap(after(shifted[0], across[0]), "row", 1))
-    across.append(swap(shifted[1], "row", 1))
-    across.append(swap(after(shifted[2], across[1]), "row", 1))
-    near = jnp.stack([other_piece] + shifted)
-    far = jnp.stack(across)
-    other_sets = [near, swap(near, "row", 0), far, swap(after(far, early), "row", 0)]
+    pieces = (own_piece, other_piece)
+    along = [ring(piece) for piece in pieces]
+    across = [[None] * cols, [None] * cols]
+    done = []
+    for which, j in ((0, 0), (0, 1), (1, 0), (0, 3), (1, 1), (0, 2), (1, 3), (1, 2)):
+        needs = done[-2:-1]
+        across[which][j] = swap(after(along[which][j], *needs), "row", 1)
+        done.append(across[which][j])
+    sets = []
+    for near, far in zip(along, across):
+        near, far = jnp.stack(near), jnp.stack(far)
+        sets.append([near, swap(near, "row", 0), far, swap(far, "row", 0)])
+    own_sets, other_sets = sets
 
     own_map = lax.dynamic_index_in_dim(child_map, cube_index, 0, keepdims=False)
     other_map = lax.dynamic_index_in_dim(child_map, cube_index ^ 1, 0, keepdims=False)
@@ -205,7 +215,7 @@
         place = jnp.stack([half_bit, position, (row ^ delta) * cols, col]).astype(jnp.int32)
         result = assemble_group(
             at, positions, cols, each, width, table, place, lefts,
-            own_set, other_sets[delta], own, other, trailing, result,
+            own_sets[delta], other_sets[delta], own, other, trailing, result,
         )
     return result[None]
 

time: 146 us -> 132 us (0.904)
  waiting for transfers between devices: 66.7 us -> 50.6 us
  between operations: 13.5 us -> 0.22 us
  starting transfers between devices: 18.4 us -> 31.4 us
  other arithmetic: 11.4 us -> 14.1 us
    ppermute x3 -> x6, starting transfers between devices: 5.51 us -> 16.7 us  [shift(): lax.ppermute(array, axis, [(i, (i + by) % extent) for i in range(extent)])]
    ppermute x10 -> x16, waiting for transfers between devices: 35.9 us -> 24.9 us  [swap(): lax.ppermute(array, axis, [(i, i ^ 1 << bit) for i in range(lax.axis_size...]
    ppermute x3 -> x6, waiting for transfers between devices: 30.5 us -> 25.7 us  [shift(): lax.ppermute(array, axis, [(i, (i + by) % extent) for i in range(extent)])]
    another operation x3 -> x5, other arithmetic: 4.7 us -> 7.18 us  [local(): near, far = (jnp.stack(near), jnp.stack(far))]
    ppermute x10 -> x16, starting transfers between devices: 12.8 us -> 14.7 us  [swap(): lax.ppermute(array, axis, [(i, i ^ 1 << bit) for i in range(lax.axis_size...]
  transfers between devices with their start and end apart: 14 -> 22, of which waited for: 9 -> 14; matrix products, arithmetic and copies ran while one was open for 9% -> 12% of each run, Pallas kernels for 15% -> 16%
where the time goes in v3:
time: 132 us
  waiting for transfers between devices  50.6 us (38%)
  starting transfers between devices  31.4 us (24%)
  Pallas kernels  28.6 us (22%)
  other arithmetic  14.1 us (11%)
  local copies, waits for them, and re-layouts  5.24 us (4%)
  matrix products  1.76 us (1%)
    pallas_call x4, Pallas kernels, assemble_group(): pl.pallas_call(kernel, grid_spec=pltpu.PrefetchScalarGridSpec(num_scalar_...  28.6 us
    ppermute x6, waiting for transfers between devices, shift(): lax.ppermute(array, axis, [(i, (i + by) % extent) for i in range(extent)])  25.7 us
    ppermute x16, waiting for transfers between devices, swap(): lax.ppermute(array, axis, [(i, i ^ 1 << bit) for i in range(lax.axis_size...  24.9 us
    ppermute x6, starting transfers between devices, shift(): lax.ppermute(array, axis, [(i, (i + by) % extent) for i in range(extent)])  16.7 us
    ppermute x16, starting transfers between devices, swap(): lax.ppermute(array, axis, [(i, i ^ 1 << bit) for i in range(lax.axis_size...  14.7 us
    another operation x5, other arithmetic, local(): near, far = (jnp.stack(near), jnp.stack(far))  7.18 us
    dynamic_slice x1, local copies, waits for them, and re-layouts, own_columns(): lax.dynamic_slice_in_dim(own, (row ^ delta) * cols * span, cols * span, 1)  3.68 us
  transfers between devices with their start and end apart: 22, of which 14 were waited for; matrix products, arithmetic and copies ran while one was open for 12% of the time, Pallas kernels for 16%

profile of v3, /device:TPU:0, one launch (start us, length us, event | category | flops | bytes accessed | tf_op | source)
XLA Modules:
  0.0 132.0 jit_solution(9201604776142466678)
XLA Ops:
  3.9 3.0 %collective-permute-start.9 = (bf16[2,384,256]{2,1,0:T(8,128)(2,1)S(1)}, bf16[2,384,256]{2,1,0:T(8,128)(2,1)S(1)}, u32[]{:S(2)}, u32[]{:S(2)}) collective-permute-start(bf16[2,384,256]{2,1,0:T(8,128)(2,1)S(1)} %get-tuple-element.30), channel_id=1, source_target_pairs={{0,16},{16,0},{1,17},{17,1},{2,18},{18,2},{3,19},{19,3},{4,20},{20... | collective-permute-start | bytes 1179656 | tf_op jit(solution)/shard_map/ppermute | solution.py:12
  7.4 3.7 %dynamic-slice_bitcast_fusion.2 = (bf16[384,1536]{1,0:T(8,128)(2,1)S(1)}, bf16[384,1536]{1,0:T(8,128)(2,1)}, bf16[384,1536]{1,0:T(8,128)(2,1)S(1)}, bf16[384,1536]{1,0:T(8,128)(2,1)S(1)}) fusion(bf16[1,384,6144]{2,1,0:T(8,128)(2,1)} %param.11, s32[]{:T(128)S(6)} %select_n.53, s32[]{:T(128)S(6)} %select_n.52, s32[]{:T(128)S(6)} %select_n.55, s32[]{:T(128)S(6)} %select_n.54), kind=kLoop, calls=%fused_computation.7 | loop fusion | bytes 9437200 | tf_op jit(solution)/shard_map/dynamic_slice | solution.py:189
  11.1 1.9 %pad_maximum_fusion = bf16[384,4608]{1,0:T(8,128)(2,1)} fusion(bf16[384,1536]{1,0:T(8,128)(2,1)S(1)} %get-tuple-element.27, bf16[384,1536]{1,0:T(8,128)(2,1)S(1)} %get-tuple-element.28, bf16[384,1536]{1,0:T(8,128)(2,1)S(1)} %get-tuple-element.25), kind=kLoop, calls=%fused_computation | loop fusion | flops 10616832 | bytes 7077888 | tf_op jit(solution)/shard_map/concatenate | solution.py:190
  13.0 7.3 %collective-permute-done = bf16[384,256]{1,0:T(8,128)(2,1)S(1)} collective-permute-done((bf16[384,256]{1,0:T(8,128)(2,1)S(1)}, bf16[384,256]{1,0:T(8,128)(2,1)S(1)}, u32[]{:S(2)}, u32[]{:S(2)}) %collective-permute-start) | collective-permute-done | bytes 196640 | tf_op jit(solution)/shard_map/ppermute | solution.py:12
  20.3 1.7 %collective-permute-start.19 = (bf16[384,4608]{1,0:T(8,128)(2,1)}, bf16[384,4608]{1,0:T(8,128)(2,1)}, u32[]{:S(2)}, u32[]{:S(2)}) collective-permute-start(bf16[384,4608]{1,0:T(8,128)(2,1)} %pad_maximum_fusion), channel_id=1, source_target_pairs={{0,16},{16,0},{1,17},{17,1},{2,18},{18,2},{3,19},{19,3},{4,20},{20... | collective-permute-start | bytes 10616840 | tf_op jit(solution)/shard_map/ppermute | solution.py:12
  22.0 1.6 %collective-permute-start.2 = (bf16[2,384,256]{2,1,0:T(8,128)(2,1)S(1)}, bf16[2,384,256]{2,1,0:T(8,128)(2,1)S(1)}, u32[]{:S(2)}, u32[]{:S(2)}) collective-permute-start(bf16[2,384,256]{2,1,0:T(8,128)(2,1)S(1)} %get-tuple-element.30), channel_id=1, source_target_pairs={{0,1},{1,2},{2,3},{3,0},{4,5},{5,6},{6,7},{7,4},{8,9},{9,10},{10,1... | collective-permute-start | bytes 1179656 | tf_op jit(solution)/shard_map/ppermute | solution.py:17
  23.6 1.5 %collective-permute-start.1 = (bf16[2,384,256]{2,1,0:T(8,128)(2,1)S(1)}, bf16[2,384,256]{2,1,0:T(8,128)(2,1)S(1)}, u32[]{:S(2)}, u32[]{:S(2)}) collective-permute-start(bf16[2,384,256]{2,1,0:T(8,128)(2,1)S(1)} %get-tuple-element.30), channel_id=1, source_target_pairs={{0,8},{4,12},{8,0},{12,4},{1,9},{5,13},{9,1},{13,5},{2,10},{6,14},... | collective-permute-start | bytes 1179656 | tf_op jit(solution)/shard_map/ppermute | solution.py:12
  25.1 2.2 %collective-permute-start.5 = (bf16[2,384,256]{2,1,0:T(8,128)(2,1)S(1)}, bf16[2,384,256]{2,1,0:T(8,128)(2,1)S(1)}, u32[]{:S(2)}, u32[]{:S(2)}) collective-permute-start(bf16[2,384,256]{2,1,0:T(8,128)(2,1)S(1)} %get-tuple-element.30), channel_id=1, source_target_pairs={{0,3},{1,0},{2,1},{3,2},{4,7},{5,4},{6,5},{7,6},{8,11},{9,8},{10,9... | collective-permute-start | bytes 1179656 | tf_op jit(solution)/shard_map/ppermute | solution.py:17
  27.3 8.6 %collective-permute-done.2 = bf16[2,384,256]{2,1,0:T(8,128)(2,1)S(1)} collective-permute-done((bf16[2,384,256]{2,1,0:T(8,128)(2,1)S(1)}, bf16[2,384,256]{2,1,0:T(8,128)(2,1)S(1)}, u32[]{:S(2)}, u32[]{:S(2)}) %collective-permute-start.2) | collective-permute-done | bytes 393248 | tf_op jit(solution)/shard_map/ppermute | solution.py:17
  35.9 1.5 %collective-permute-start.3 = (bf16[2,384,256]{2,1,0:T(8,128)(2,1)S(1)}, bf16[2,384,256]{2,1,0:T(8,128)(2,1)}, u32[]{:S(2)}, u32[]{:S(2)}) collective-permute-start(bf16[2,384,256]{2,1,0:T(8,128)(2,1)S(1)} %collective-permute-done.2), channel_id=1, source_target_pairs={{0,8},{4,12},{8,0},{12,4},{1,9},{5,13},{9,1},{13,5},{2,10},{6,14},... | collective-permute-start | bytes 1179656 | tf_op jit(solution)/shard_map/ppermute | solution.py:12
  37.4 3.0 %collective-permute-start.11 = (bf16[2,384,256]{2,1,0:T(8,128)(2,1)S(1)}, bf16[2,384,256]{2,1,0:T(8,128)(2,1)S(1)}, u32[]{:S(2)}, u32[]{:S(2)}) collective-permute-start(bf16[2,384,256]{2,1,0:T(8,128)(2,1)S(1)} %collective-permute-done.9), channel_id=1, source_target_pairs={{0,1},{1,2},{2,3},{3,0},{4,5},{5,6},{6,7},{7,4},{8,9},{9,10},{10,1... | collective-permute-start | bytes 1179656 | tf_op jit(solution)/shard_map/ppermute | solution.py:17
  40.4 3.8 %collective-permute-done.5 = bf16[2,384,256]{2,1,0:T(8,128)(2,1)S(1)} collective-permute-done((bf16[2,384,256]{2,1,0:T(8,128)(2,1)S(1)}, bf16[2,384,256]{2,1,0:T(8,128)(2,1)S(1)}, u32[]{:S(2)}, u32[]{:S(2)}) %collective-permute-start.5) | collective-permute-done | bytes 393248 | tf_op jit(solution)/shard_map/ppermute | solution.py:17
  44.8 2.0 %collective-permute-done.3 = bf16[2,384,256]{2,1,0:T(8,128)(2,1)} collective-permute-done((bf16[2,384,256]{2,1,0:T(8,128)(2,1)S(1)}, bf16[2,384,256]{2,1,0:T(8,128)(2,1)}, u32[]{:S(2)}, u32[]{:S(2)}) %collective-permute-start.3) | collective-permute-done | bytes 393248 | tf_op jit(solution)/shard_map/ppermute | solution.py:12
  46.8 1.5 %collective-permute-start.6 = (bf16[2,384,256]{2,1,0:T(8,128)(2,1)S(1)}, bf16[2,384,256]{2,1,0:T(8,128)(2,1)S(1)}, u32[]{:S(2)}, u32[]{:S(2)}) collective-permute-start(bf16[2,384,256]{2,1,0:T(8,128)(2,1)S(1)} %collective-permute-done.5), channel_id=1, source_target_pairs={{0,8},{4,12},{8,0},{12,4},{1,9},{5,13},{9,1},{13,5},{2,10},{6,14},... | collective-permute-start | bytes 1179656 | tf_op jit(solution)/shard_map/ppermute | solution.py:12
  48.3 4.2 %collective-permute-done.11 = bf16[2,384,256]{2,1,0:T(8,128)(2,1)S(1)} collective-permute-done((bf16[2,384,256]{2,1,0:T(8,128)(2,1)S(1)}, bf16[2,384,256]{2,1,0:T(8,128)(2,1)S(1)}, u32[]{:S(2)}, u32[]{:S(2)}) %collective-permute-start.11) | collective-permute-done | bytes 393248 | tf_op jit(solution)/shard_map/ppermute | solution.py:17
  52.5 3.9 %collective-permute-start.15 = (bf16[2,384,256]{2,1,0:T(8,128)(2,1)S(1)}, bf16[2,384,256]{2,1,0:T(8,128)(2,1)}, u32[]{:S(2)}, u32[]{:S(2)}) collective-permute-start(bf16[2,384,256]{2,1,0:T(8,128)(2,1)S(1)} %collective-permute-done.9), channel_id=1, source_target_pairs={{0,3},{1,0},{2,1},{3,2},{4,7},{5,4},{6,5},{7,6},{8,11},{9,8},{10,9... | collective-permute-start | bytes 1179656 | tf_op jit(solution)/shard_map/ppermute | solution.py:17
  57.4 3.5 %collective-permute-done.4 = bf16[2,384,256]{2,1,0:T(8,128)(2,1)} collective-permute-done((bf16[2,384,256]{2,1,0:T(8,128)(2,1)S(1)}, bf16[2,384,256]{2,1,0:T(8,128)(2,1)}, u32[]{:S(2)}, u32[]{:S(2)}) %collective-permute-start.4) | collective-permute-done | bytes 393248 | tf_op jit(solution)/shard_map/ppermute | solution.py:17
  60.9 5.4 %collective-permute-start.13 = (bf16[2,384,256]{2,1,0:T(8,128)(2,1)S(1)}, bf16[2,384,256]{2,1,0:T(8,128)(2,1)}, u32[]{:S(2)}, u32[]{:S(2)}) collective-permute-start(bf16[2,384,256]{2,1,0:T(8,128)(2,1)S(1)} %collective-permute-done.11), channel_id=1, source_target_pairs={{0,1},{1,2},{2,3},{3,0},{4,5},{5,6},{6,7},{7,4},{8,9},{9,10},{10,1... | collective-permute-start | bytes 1179656 | tf_op jit(solution)/shard_map/ppermute | solution.py:17
  67.0 2.2 %collective-permute-done.15 = bf16[2,384,256]{2,1,0:T(8,128)(2,1)} collective-permute-done((bf16[2,384,256]{2,1,0:T(8,128)(2,1)S(1)}, bf16[2,384,256]{2,1,0:T(8,128)(2,1)}, u32[]{:S(2)}, u32[]{:S(2)}) %collective-permute-start.15) | collective-permute-done | bytes 393248 | tf_op jit(solution)/shard_map/ppermute | solution.py:17
  69.2 2.2 %collective-permute-done.12 = bf16[2,384,256]{2,1,0:T(8,128)(2,1)S(1)} collective-permute-done((bf16[2,384,256]{2,1,0:T(8,128)(2,1)S(1)}, bf16[2,384,256]{2,1,0:T(8,128)(2,1)S(1)}, u32[]{:S(2)}, u32[]{:S(2)}) %collective-permute-start.12) | collective-permute-done | bytes 393248 | tf_op jit(solution)/shard_map/ppermute | solution.py:12
  71.4 1.6 %collective-permute-start.16 = (bf16[2,384,256]{2,1,0:T(8,128)(2,1)}, bf16[2,384,256]{2,1,0:T(8,128)(2,1)S(1)}, u32[]{:S(2)}, u32[]{:S(2)}) collective-permute-start(bf16[2,384,256]{2,1,0:T(8,128)(2,1)} %collective-permute-done.15), channel_id=1, source_target_pairs={{0,8},{4,12},{8,0},{12,4},{1,9},{5,13},{9,1},{13,5},{2,10},{6,14},... | collective-permute-start | bytes 1179656 | tf_op jit(solution)/shard_map/ppermute | solution.py:12
  73.0 3.4 %collective-permute-done.13 = bf16[2,384,256]{2,1,0:T(8,128)(2,1)} collective-permute-done((bf16[2,384,256]{2,1,0:T(8,128)(2,1)S(1)}, bf16[2,384,256]{2,1,0:T(8,128)(2,1)}, u32[]{:S(2)}, u32[]{:S(2)}) %collective-permute-start.13) | collective-permute-done | bytes 393248 | tf_op jit(solution)/shard_map/ppermute | solution.py:17
  76.4 3.5 %collective-permute-done.7 = bf16[2,384,256]{2,1,0:T(8,128)(2,1)} collective-permute-done((bf16[2,384,256]{2,1,0:T(8,128)(2,1)}, bf16[2,384,256]{2,1,0:T(8,128)(2,1)}, u32[]{:S(2)}, u32[]{:S(2)}) %collective-permute-start.7) | collective-permute-done | bytes 393248 | tf_op jit(solution)/shard_map/ppermute | solution.py:12
  79.9 1.6 %collective-permute-start.14 = (bf16[2,384,256]{2,1,0:T(8,128)(2,1)}, bf16[2,384,256]{2,1,0:T(8,128)(2,1)S(1)}, u32[]{:S(2)}, u32[]{:S(2)}) collective-permute-start(bf16[2,384,256]{2,1,0:T(8,128)(2,1)} %collective-permute-done.13), channel_id=1, source_target_pairs={{0,8},{4,12},{8,0},{12,4},{1,9},{5,13},{9,1},{13,5},{2,10},{6,14},... | collective-permute-start | bytes 1179656 | tf_op jit(solution)/shard_map/ppermute | solution.py:12
  83.0 3.0 %pad_maximum_fusion.4.other_set_ref = bf16[4,2,384,256]{3,2,1,0:T(8,128)(2,1)} fusion(bf16[1,2,384,256]{3,2,1,0:T(8,128)(2,1)} %bitcast.40, bf16[1,2,384,256]{3,2,1,0:T(8,128)(2,1)} %bitcast.39, bf16[1,2,384,256]{3,2,1,0:T(8,128)(2,1)S(1)} %bitcast.79, bf16[1,2,384,256]{3,2,1,0:T(8,128)(2,1)S(1)} %bitcast.74), kind=kLoop, calls=%fused_computation.4 | loop fusion | flops 2359296 | bytes 3145728 | tf_op jit(solution)/shard_map/stack | solution.py:205
  88.3 4.8 %collective-permute-done.14 = bf16[2,384,256]{2,1,0:T(8,128)(2,1)S(1)} collective-permute-done((bf16[2,384,256]{2,1,0:T(8,128)(2,1)}, bf16[2,384,256]{2,1,0:T(8,128)(2,1)S(1)}, u32[]{:S(2)}, u32[]{:S(2)}) %collective-permute-start.14) | collective-permute-done | bytes 393248 | tf_op jit(solution)/shard_map/ppermute | solution.py:12
  94.5 3.8 %collective-permute-done.19.other_ref = bf16[384,4608]{1,0:T(8,128)(2,1)} collective-permute-done((bf16[384,4608]{1,0:T(8,128)(2,1)}, bf16[384,4608]{1,0:T(8,128)(2,1)}, u32[]{:S(2)}, u32[]{:S(2)}) %collective-permute-start.19) | collective-permute-done | bytes 3538976 | tf_op jit(solution)/shard_map/ppermute | solution.py:12
  98.3 1.4 %collective-permute-start.18 = (bf16[384,1536]{1,0:T(8,128)(2,1)}, bf16[384,1536]{1,0:T(8,128)(2,1)}, u32[]{:S(2)}, u32[]{:S(2)}) collective-permute-start(bf16[384,1536]{1,0:T(8,128)(2,1)} %get-tuple-element.26), channel_id=1, source_target_pairs={{0,16},{16,0},{1,17},{17,1},{2,18},{18,2},{3,19},{19,3},{4,20},{20... | collective-permute-start | bytes 3538952 | tf_op jit(solution)/shard_map/ppermute | solution.py:12
  102.6 7.3 %assemble.4.rest_0_ = bf16[384,12288]{1,0:T(8,128)(2,1)} custom-call(s32[192]{0:T(256)S(1)} %reshape.96.table_ref, s32[4]{0:T(128)S(1)} %get-tuple-element.23.place_ref, bf16[3,384,256]{2,1,0:T(8,128)(2,1)S(1)} %pad_maximum_fusion.5.lefts_ref, bf16[4,2,384,256]{3,2,1,0:T(8,128)(2,1)} %copy-done.2, bf16[4,2,384,256]{3,2,1,0:T(8,128)(2,1)} %pad_maximum_fusion.4.other_set_ref, ...), custom_call_target="tpu_custom_call" | custom-call | flops 1207959552 | bytes 10813440 | tf_op jit(solution)/shard_map/assemble/pallas_call | solution.py:128
  109.9 7.1 %assemble.5.rest_0_ = bf16[384,12288]{1,0:T(8,128)(2,1)} custom-call(s32[192]{0:T(256)S(1)} %reshape.96.table_ref, s32[4]{0:T(128)S(1)} %get-tuple-element.31.place_ref, bf16[3,384,256]{2,1,0:T(8,128)(2,1)S(1)} %pad_maximum_fusion.5.lefts_ref, bf16[4,2,384,256]{3,2,1,0:T(8,128)(2,1)} %collective-permute-done.20.own_set_ref, ...), custom_call_target="tpu_custom_call", output_to_operand_aliasing={{}: (8, {})} | custom-call | flops 1207959552 | bytes 10813440 | tf_op jit(solution)/shard_map/assemble/pallas_call | solution.py:128
  117.1 7.1 %assemble.6.rest_0_ = bf16[384,12288]{1,0:T(8,128)(2,1)} custom-call(s32[192]{0:T(256)S(1)} %reshape.96.table_ref, s32[4]{0:T(128)S(1)} %get-tuple-element.32.place_ref, bf16[3,384,256]{2,1,0:T(8,128)(2,1)S(1)} %pad_maximum_fusion.5.lefts_ref, bf16[4,2,384,256]{3,2,1,0:T(8,128)(2,1)} %copy-done.1, ...), custom_call_target="tpu_custom_call", output_to_operand_aliasing={{}: (8, {})} | custom-call | flops 1207959552 | bytes 10813440 | tf_op jit(solution)/shard_map/assemble/pallas_call | solution.py:128
  124.9 7.1 %assemble.7 = bf16[384,12288]{1,0:T(8,128)(2,1)} custom-call(s32[192]{0:T(256)S(1)} %reshape.96.table_ref, s32[4]{0:T(128)S(1)} %get-tuple-element.33.place_ref, bf16[3,384,256]{2,1,0:T(8,128)(2,1)S(1)} %pad_maximum_fusion.5.lefts_ref, bf16[4,2,384,256]{3,2,1,0:T(8,128)(2,1)} %collective-permute-done.8.own_set_ref, ...), custom_call_target="tpu_custom_call", output_to_operand_aliasing={{}: (8, {})} | custom-call | flops 1207959552 | bytes 10813440 | tf_op jit(solution)/shard_map/assemble/pallas_call | solution.py:128
  (82 shorter events, 15.4 us)
Async XLA Ops:
  0.0 6.9 %copy-start = (f32[1,256,256]{2,1,0:T(8,128)S(1)}, f32[1,256,256]{2,1,0:T(8,128)}, u32[]{:S(2)}) copy-start(f32[1,256,256]{2,1,0:T(8,128)} %param.10) | copy-start | bytes 786436
  3.9 16.4 %collective-permute-start.9 = (bf16[2,384,256]{2,1,0:T(8,128)(2,1)S(1)}, bf16[2,384,256]{2,1,0:T(8,128)(2,1)S(1)}, u32[]{:S(2)}, u32[]{:S(2)}) collective-permute-start(bf16[2,384,256]{2,1,0:T(8,128)(2,1)S(1)} %get-tuple-element.30), channel_id=1, source_target_pairs={{0,16},{16,0},{1,17},{17,1},{2,18},{18,2},{3,19},{19,3},{4,20},{20... | collective-permute-start | bytes 1179656 | tf_op jit(solution)/shard_map/ppermute | solution.py:12
  7.3 13.0 %collective-permute-start = (bf16[384,256]{1,0:T(8,128)(2,1)S(1)}, bf16[384,256]{1,0:T(8,128)(2,1)S(1)}, u32[]{:S(2)}, u32[]{:S(2)}) collective-permute-start(bf16[384,256]{1,0:T(8,128)(2,1)S(1)} %convolution_convert_fusion.1), channel_id=1, source_target_pairs={{0,16},{16,0},{1,17},{17,1},{2,18},{18,2},{3,19},{19,3},{4,20},{20... | collective-permute-start | bytes 589832 | tf_op jit(solution)/shard_map/ppermute | solution.py:12
  11.1 55.6 %copy-start.17 = (s32[2,48]{1,0:T(2,128)S(1)}, s32[2,48]{1,0:T(2,128)}, u32[]{:S(2)}) copy-start(s32[2,48]{1,0:T(2,128)} %param.13) | copy-start | bytes 1156
  20.3 24.5 %copy-start.16 = (bf16[384,256]{1,0:T(8,128)(2,1)}, bf16[384,256]{1,0:T(8,128)(2,1)S(1)}, u32[]{:S(2)}) copy-start(bf16[384,256]{1,0:T(8,128)(2,1)S(1)} %collective-permute-done) | copy-start | bytes 589828
  20.3 78.0 %collective-permute-start.19 = (bf16[384,4608]{1,0:T(8,128)(2,1)}, bf16[384,4608]{1,0:T(8,128)(2,1)}, u32[]{:S(2)}, u32[]{:S(2)}) collective-permute-start(bf16[384,4608]{1,0:T(8,128)(2,1)} %pad_maximum_fusion), channel_id=1, source_target_pairs={{0,16},{16,0},{1,17},{17,1},{2,18},{18,2},{3,19},{19,3},{4,20},{20... | collective-permute-start | bytes 10616840 | tf_op jit(solution)/shard_map/ppermute | solution.py:12
  22.0 13.9 %collective-permute-start.2 = (bf16[2,384,256]{2,1,0:T(8,128)(2,1)S(1)}, bf16[2,384,256]{2,1,0:T(8,128)(2,1)S(1)}, u32[]{:S(2)}, u32[]{:S(2)}) collective-permute-start(bf16[2,384,256]{2,1,0:T(8,128)(2,1)S(1)} %get-tuple-element.30), channel_id=1, source_target_pairs={{0,1},{1,2},{2,3},{3,0},{4,5},{5,6},{6,7},{7,4},{8,9},{9,10},{10,1... | collective-permute-start | bytes 1179656 | tf_op jit(solution)/shard_map/ppermute | solution.py:17
  23.6 13.8 %collective-permute-start.1 = (bf16[2,384,256]{2,1,0:T(8,128)(2,1)S(1)}, bf16[2,384,256]{2,1,0:T(8,128)(2,1)S(1)}, u32[]{:S(2)}, u32[]{:S(2)}) collective-permute-start(bf16[2,384,256]{2,1,0:T(8,128)(2,1)S(1)} %get-tuple-element.30), channel_id=1, source_target_pairs={{0,8},{4,12},{8,0},{12,4},{1,9},{5,13},{9,1},{13,5},{2,10},{6,14},... | collective-permute-start | bytes 1179656 | tf_op jit(solution)/shard_map/ppermute | solution.py:12
  25.1 19.2 %collective-permute-start.5 = (bf16[2,384,256]{2,1,0:T(8,128)(2,1)S(1)}, bf16[2,384,256]{2,1,0:T(8,128)(2,1)S(1)}, u32[]{:S(2)}, u32[]{:S(2)}) collective-permute-start(bf16[2,384,256]{2,1,0:T(8,128)(2,1)S(1)} %get-tuple-element.30), channel_id=1, source_target_pairs={{0,3},{1,0},{2,1},{3,2},{4,7},{5,4},{6,5},{7,6},{8,11},{9,8},{10,9... | collective-permute-start | bytes 1179656 | tf_op jit(solution)/shard_map/ppermute | solution.py:17
  35.9 10.9 %collective-permute-start.3 = (bf16[2,384,256]{2,1,0:T(8,128)(2,1)S(1)}, bf16[2,384,256]{2,1,0:T(8,128)(2,1)}, u32[]{:S(2)}, u32[]{:S(2)}) collective-permute-start(bf16[2,384,256]{2,1,0:T(8,128)(2,1)S(1)} %collective-permute-done.2), channel_id=1, source_target_pairs={{0,8},{4,12},{8,0},{12,4},{1,9},{5,13},{9,1},{13,5},{2,10},{6,14},... | collective-permute-start | bytes 1179656 | tf_op jit(solution)/shard_map/ppermute | solution.py:12
  37.4 45.5 %copy-start.5 = (bf16[2,384,256]{2,1,0:T(8,128)(2,1)}, bf16[2,384,256]{2,1,0:T(8,128)(2,1)S(1)}, u32[]{:S(2)}) copy-start(bf16[2,384,256]{2,1,0:T(8,128)(2,1)S(1)} %collective-permute-done.1) | copy-start | bytes 1179652
  37.4 15.1 %collective-permute-start.11 = (bf16[2,384,256]{2,1,0:T(8,128)(2,1)S(1)}, bf16[2,384,256]{2,1,0:T(8,128)(2,1)S(1)}, u32[]{:S(2)}, u32[]{:S(2)}) collective-permute-start(bf16[2,384,256]{2,1,0:T(8,128)(2,1)S(1)} %collective-permute-done.9), channel_id=1, source_target_pairs={{0,1},{1,2},{2,3},{3,0},{4,5},{5,6},{6,7},{7,4},{8,9},{9,10},{10,1... | collective-permute-start | bytes 1179656 | tf_op jit(solution)/shard_map/ppermute | solution.py:17
  40.4 16.0 %collective-permute-start.10 = (bf16[2,384,256]{2,1,0:T(8,128)(2,1)S(1)}, bf16[2,384,256]{2,1,0:T(8,128)(2,1)S(1)}, u32[]{:S(2)}, u32[]{:S(2)}) collective-permute-start(bf16[2,384,256]{2,1,0:T(8,128)(2,1)S(1)} %collective-permute-done.9), channel_id=1, source_target_pairs={{0,8},{4,12},{8,0},{12,4},{1,9},{5,13},{9,1},{13,5},{2,10},{6,14},... | collective-permute-start | bytes 1179656 | tf_op jit(solution)/shard_map/ppermute | solution.py:12
  44.2 37.3 %copy-start.9 = (bf16[2,384,256]{2,1,0:T(8,128)(2,1)}, bf16[2,384,256]{2,1,0:T(8,128)(2,1)S(1)}, u32[]{:S(2)}) copy-start(bf16[2,384,256]{2,1,0:T(8,128)(2,1)S(1)} %collective-permute-done.5) | copy-start | bytes 1179652
  44.2 16.6 %collective-permute-start.4 = (bf16[2,384,256]{2,1,0:T(8,128)(2,1)S(1)}, bf16[2,384,256]{2,1,0:T(8,128)(2,1)}, u32[]{:S(2)}, u32[]{:S(2)}) collective-permute-start(bf16[2,384,256]{2,1,0:T(8,128)(2,1)S(1)} %collective-permute-done.2), channel_id=1, source_target_pairs={{0,1},{1,2},{2,3},{3,0},{4,5},{5,6},{6,7},{7,4},{8,9},{9,10},{10,1... | collective-permute-start | bytes 1179656 | tf_op jit(solution)/shard_map/ppermute | solution.py:17
  46.8 19.6 %collective-permute-start.6 = (bf16[2,384,256]{2,1,0:T(8,128)(2,1)S(1)}, bf16[2,384,256]{2,1,0:T(8,128)(2,1)S(1)}, u32[]{:S(2)}, u32[]{:S(2)}) collective-permute-start(bf16[2,384,256]{2,1,0:T(8,128)(2,1)S(1)} %collective-permute-done.5), channel_id=1, source_target_pairs={{0,8},{4,12},{8,0},{12,4},{1,9},{5,13},{9,1},{13,5},{2,10},{6,14},... | collective-permute-start | bytes 1179656 | tf_op jit(solution)/shard_map/ppermute | solution.py:12
  52.5 29.0 %copy-start.10 = (bf16[2,384,256]{2,1,0:T(8,128)(2,1)}, bf16[2,384,256]{2,1,0:T(8,128)(2,1)S(1)}, u32[]{:S(2)}) copy-start(bf16[2,384,256]{2,1,0:T(8,128)(2,1)S(1)} %collective-permute-done.11) | copy-start | bytes 1179652
  52.5 16.8 %collective-permute-start.15 = (bf16[2,384,256]{2,1,0:T(8,128)(2,1)S(1)}, bf16[2,384,256]{2,1,0:T(8,128)(2,1)}, u32[]{:S(2)}, u32[]{:S(2)}) collective-permute-start(bf16[2,384,256]{2,1,0:T(8,128)(2,1)S(1)} %collective-permute-done.9), channel_id=1, source_target_pairs={{0,3},{1,0},{2,1},{3,2},{4,7},{5,4},{6,5},{7,6},{8,11},{9,8},{10,9... | collective-permute-start | bytes 1179656 | tf_op jit(solution)/shard_map/ppermute | solution.py:17
  57.1 14.3 %collective-permute-start.12 = (bf16[2,384,256]{2,1,0:T(8,128)(2,1)S(1)}, bf16[2,384,256]{2,1,0:T(8,128)(2,1)S(1)}, u32[]{:S(2)}, u32[]{:S(2)}) collective-permute-start(bf16[2,384,256]{2,1,0:T(8,128)(2,1)S(1)} %collective-permute-done.11), channel_id=1, source_target_pairs={{0,8},{4,12},{8,0},{12,4},{1,9},{5,13},{9,1},{13,5},{2,10},{6,14},... | collective-permute-start | bytes 1179656 | tf_op jit(solution)/shard_map/ppermute | solution.py:12
  60.9 15.5 %collective-permute-start.13 = (bf16[2,384,256]{2,1,0:T(8,128)(2,1)S(1)}, bf16[2,384,256]{2,1,0:T(8,128)(2,1)}, u32[]{:S(2)}, u32[]{:S(2)}) collective-permute-start(bf16[2,384,256]{2,1,0:T(8,128)(2,1)S(1)} %collective-permute-done.11), channel_id=1, source_target_pairs={{0,1},{1,2},{2,3},{3,0},{4,5},{5,6},{6,7},{7,4},{8,9},{9,10},{10,1... | collective-permute-start | bytes 1179656 | tf_op jit(solution)/shard_map/ppermute | solution.py:17
  66.3 15.2 %copy-start.14 = (bf16[2,384,256]{2,1,0:T(8,128)(2,1)}, bf16[2,384,256]{2,1,0:T(8,128)(2,1)S(1)}, u32[]{:S(2)}) copy-start(bf16[2,384,256]{2,1,0:T(8,128)(2,1)S(1)} %collective-permute-done.6) | copy-start | bytes 1179652
  66.3 13.6 %collective-permute-start.7 = (bf16[2,384,256]{2,1,0:T(8,128)(2,1)}, bf16[2,384,256]{2,1,0:T(8,128)(2,1)}, u32[]{:S(2)}, u32[]{:S(2)}) collective-permute-start(bf16[2,384,256]{2,1,0:T(8,128)(2,1)} %collective-permute-done.4), channel_id=1, source_target_pairs={{0,8},{4,12},{8,0},{12,4},{1,9},{5,13},{9,1},{13,5},{2,10},{6,14},... | collective-permute-start | bytes 1179656 | tf_op jit(solution)/shard_map/ppermute | solution.py:12
  71.4 10.1 %copy-start.12 = (bf16[2,384,256]{2,1,0:T(8,128)(2,1)}, bf16[2,384,256]{2,1,0:T(8,128)(2,1)S(1)}, u32[]{:S(2)}) copy-start(bf16[2,384,256]{2,1,0:T(8,128)(2,1)S(1)} %collective-permute-done.12) | copy-start | bytes 1179652
  71.4 16.9 %collective-permute-start.16 = (bf16[2,384,256]{2,1,0:T(8,128)(2,1)}, bf16[2,384,256]{2,1,0:T(8,128)(2,1)S(1)}, u32[]{:S(2)}, u32[]{:S(2)}) collective-permute-start(bf16[2,384,256]{2,1,0:T(8,128)(2,1)} %collective-permute-done.15), channel_id=1, source_target_pairs={{0,8},{4,12},{8,0},{12,4},{1,9},{5,13},{9,1},{13,5},{2,10},{6,14},... | collective-permute-start | bytes 1179656 | tf_op jit(solution)/shard_map/ppermute | solution.py:12
  79.9 13.1 %collective-permute-start.14 = (bf16[2,384,256]{2,1,0:T(8,128)(2,1)}, bf16[2,384,256]{2,1,0:T(8,128)(2,1)S(1)}, u32[]{:S(2)}, u32[]{:S(2)}) collective-permute-start(bf16[2,384,256]{2,1,0:T(8,128)(2,1)} %collective-permute-done.13), channel_id=1, source_target_pairs={{0,8},{4,12},{8,0},{12,4},{1,9},{5,13},{9,1},{13,5},{2,10},{6,14},... | collective-permute-start | bytes 1179656 | tf_op jit(solution)/shard_map/ppermute | solution.py:12
  82.9 27.0 %collective-permute-start.20 = (bf16[4,2,384,256]{3,2,1,0:T(8,128)(2,1)S(1)}, bf16[4,2,384,256]{3,2,1,0:T(8,128)(2,1)}, u32[]{:S(2)}, u32[]{:S(2)}) collective-permute-start(bf16[4,2,384,256]{3,2,1,0:T(8,128)(2,1)S(1)} %pad_maximum_fusion.3.own_set_ref), channel_id=1, source_target_pairs={{0,4},{4,0},{8,12},{12,8},{1,5},{5,1},{9,13},{13,9},{2,6},{6,2},{1... | collective-permute-start | bytes 4718600 | tf_op jit(solution)/shard_map/ppermute | solution.py:12
  86.0 23.9 %collective-permute-start.21 = (bf16[4,2,384,256]{3,2,1,0:T(8,128)(2,1)}, bf16[4,2,384,256]{3,2,1,0:T(8,128)(2,1)}, u32[]{:S(2)}, u32[]{:S(2)}) collective-permute-start(bf16[4,2,384,256]{3,2,1,0:T(8,128)(2,1)} %pad_maximum_fusion.4.other_set_ref), channel_id=1, source_target_pairs={{0,4},{4,0},{8,12},{12,8},{1,5},{5,1},{9,13},{13,9},{2,6},{6,2},{1... | collective-permute-start | bytes 4718600 | tf_op jit(solution)/shard_map/ppermute | solution.py:12
  86.1 6.9 %copy-start.8 = (bf16[2,384,256]{2,1,0:T(8,128)(2,1)S(1)}, bf16[2,384,256]{2,1,0:T(8,128)(2,1)}, u32[]{:S(2)}) copy-start(bf16[2,384,256]{2,1,0:T(8,128)(2,1)} %copy-done.7) | copy-start | bytes 1179652
  86.1 6.9 %copy-start.13 = (bf16[2,384,256]{2,1,0:T(8,128)(2,1)S(1)}, bf16[2,384,256]{2,1,0:T(8,128)(2,1)}, u32[]{:S(2)}) copy-start(bf16[2,384,256]{2,1,0:T(8,128)(2,1)} %copy-done.12) | copy-start | bytes 1179652
  88.3 36.6 %collective-permute-start.8 = (bf16[4,2,384,256]{3,2,1,0:T(8,128)(2,1)S(1)}, bf16[4,2,384,256]{3,2,1,0:T(8,128)(2,1)}, u32[]{:S(2)}, u32[]{:S(2)}) collective-permute-start(bf16[4,2,384,256]{3,2,1,0:T(8,128)(2,1)S(1)} %pad_maximum_fusion.1.own_set_ref), channel_id=1, source_target_pairs={{0,4},{4,0},{8,12},{12,8},{1,5},{5,1},{9,13},{13,9},{2,6},{6,2},{1... | collective-permute-start | bytes 4718600 | tf_op jit(solution)/shard_map/ppermute | solution.py:12
  94.4 30.5 %collective-permute-start.17 = (bf16[4,2,384,256]{3,2,1,0:T(8,128)(2,1)}, bf16[4,2,384,256]{3,2,1,0:T(8,128)(2,1)}, u32[]{:S(2)}, u32[]{:S(2)}) collective-permute-start(bf16[4,2,384,256]{3,2,1,0:T(8,128)(2,1)} %pad_maximum_fusion.2.other_set_ref), channel_id=1, source_target_pairs={{0,4},{4,0},{8,12},{12,8},{1,5},{5,1},{9,13},{13,9},{2,6},{6,2},{1... | collective-permute-start | bytes 4718600 | tf_op jit(solution)/shard_map/ppermute | solution.py:12
  98.3 26.5 %collective-permute-start.18 = (bf16[384,1536]{1,0:T(8,128)(2,1)}, bf16[384,1536]{1,0:T(8,128)(2,1)}, u32[]{:S(2)}, u32[]{:S(2)}) collective-permute-start(bf16[384,1536]{1,0:T(8,128)(2,1)} %get-tuple-element.26), channel_id=1, source_target_pairs={{0,16},{16,0},{1,17},{17,1},{2,18},{18,2},{3,19},{19,3},{4,20},{20... | collective-permute-start | bytes 3538952 | tf_op jit(solution)/shard_map/ppermute | solution.py:12
  (8 other events, 23.4 us)

commit v4 on v3

--- a/solution.py
+++ b/solution.py
@@ -17,10 +17,29 @@
     return lax.ppermute(array, axis, [(i, (i + by) % extent) for i in range(extent)])
 
 
-def masked_rows(panel, pattern_row, start):
-    blocks = panel.shape[0] // BLOCK
-    window = lax.dynamic_slice_in_dim(pattern_row, start, blocks)
-    return panel * jnp.repeat(window, BLOCK).astype(panel.dtype)[:, None]
+def masked_pair(child, parent, child_pattern, parent_pattern, starts):
+    rows, pivots = child.shape
+    blocks = rows // BLOCK
+
+    def kernel(starts_ref, child_pattern_ref, parent_pattern_ref, child_ref, parent_ref, out_ref):
+        for i in range(blocks):
+            at = slice(i * BLOCK, (i + 1) * BLOCK)
+            for which, (source_ref, flag) in enumerate((
+                (child_ref, child_pattern_ref[0, starts_ref[0] + i]),
+                (parent_ref, parent_pattern_ref[starts_ref[1], starts_ref[2] + i]),
+            )):
+                here = source_ref[at]
+                out_ref[which, at] = jnp.where(flag != 0, here, jnp.zeros_like(here))
+
+    smem = pl.BlockSpec(memory_space=pltpu.SMEM)
+    vmem = pl.BlockSpec(memory_space=pltpu.VMEM)
+    return pl.pallas_call(
+        kernel,
+        in_specs=[smem, smem, smem, vmem, vmem],
+        out_specs=vmem,
+        out_shape=jax.ShapeDtypeStruct((2, rows, pivots), jnp.bfloat16),
+        name="masked",
+    )(starts, child_pattern, parent_pattern, child, parent)
 
 
 def left_factor(masked, inverse):
@@ -118,7 +137,7 @@
         pl.BlockSpec((rows, cols * span), lambda h, t, p: (0, at)),
         pl.BlockSpec((rows, cols * wide), lambda h, t, p: (0, h * halves + p[2] // cols)),
     ]
-    operands = [lefts, in_hbm(own_set), in_hbm(other_set), in_hbm(own), in_hbm(other), in_hbm(trailing)]
+    operands = [lefts, own_set, other_set, in_hbm(own), other, in_hbm(trailing)]
     aliases = {}
     if previous is not None:
         in_specs.append(pl.BlockSpec(memory_space=pl.ANY))
@@ -174,10 +193,9 @@
     rows = own.shape[0]
     span = each * BLOCK
 
-    own_child = masked_rows(child_panel[0], child_pattern[0], position * each)
-    pattern_row = lax.dynamic_index_in_dim(parent_pattern, parent, 0, keepdims=False)
-    own_parent = masked_rows(parent_panel[0], pattern_row, half_bit * (parent_blocks // 2) + position * width)
-    own_piece = jnp.stack([own_child, own_parent])
+    starts = jnp.stack([position * each, parent, half_bit * (parent_blocks // 2) + position * width]).astype(jnp.int32)
+    own_piece = masked_pair(child_panel[0], parent_panel[0], child_pattern, parent_pattern, starts)
+    own_child, own_parent = own_piece[0], own_piece[1]
     other_piece = swap(own_piece, "cube", 0)
 
     child_left = left_factor(own_child, child_inverse[0])
@@ -197,7 +215,7 @@
     across = [[None] * cols, [None] * cols]
     done = []
     for which, j in ((0, 0), (0, 1), (1, 0), (0, 3), (1, 1), (0, 2), (1, 3), (1, 2)):
-        needs = done[-2:-1]
+        needs = done[-2:-1] + ([lefts] if (which, j) == (1, 2) else [])
         across[which][j] = swap(after(along[which][j], *needs), "row", 1)
         done.append(across[which][j])
     sets = []

time: 132 us -> 131 us (level)
  other arithmetic: 14.1 us -> 5.49 us
  waiting for transfers between devices: 50.6 us -> 57.4 us
    ppermute x16, waiting for transfers between devices: 24.9 us -> 31.2 us  [swap(): lax.ppermute(array, axis, [(i, i ^ 1 << bit) for i in range(lax.axis_size...]
    another operation x5 -> x4, other arithmetic: 7.18 us -> 4.27 us  [local(): near, far = (jnp.stack(near), jnp.stack(far))]
    mul x2 -> x0, other arithmetic: 2.15 us -> none  [masked_rows(): return panel * jnp.repeat(window, BLOCK).astype(panel.dtype)[:, None]]
    pallas_call x0 -> x1, Pallas kernels: none -> 1.81 us  [masked_pair(): pl.pallas_call(kernel, in_specs=[smem, smem, smem, vmem, vmem], out_specs...]
    concatenate x1, other arithmetic: 1.9 us -> 0.25 us  [own_columns(): return parts[0] if len(parts) == 1 else jnp.concatenate(parts, axis=1)]
    convert_element_type x2 -> x0, other arithmetic: 1.5 us -> none  [masked_rows(): return panel * jnp.repeat(window, BLOCK).astype(panel.dtype)[:, None]]
  transfers between devices with their start and end apart: 22 -> 22, of which waited for: 14 -> 14; matrix products, arithmetic and copies ran while one was open for 12% -> 8% of each run, Pallas kernels for 16% -> 16%
where the time goes in v4:
time: 131 us; the launch traced here: 130 us
  waiting for transfers between devices  57.4 us (44%)
  starting transfers between devices  31.7 us (24%)
  Pallas kernels  29.7 us (23%)
  other arithmetic  5.49 us (4%)
  local copies, waits for them, and re-layouts  4.31 us (3%)
  matrix products  1.67 us (1%)
    ppermute x16, waiting for transfers between devices, swap(): lax.ppermute(array, axis, [(i, i ^ 1 << bit) for i in range(lax.axis_size...  31.2 us
    pallas_call x4, Pallas kernels, assemble_group(): pl.pallas_call(kernel, grid_spec=pltpu.PrefetchScalarGridSpec(num_scalar_...  27.9 us
    ppermute x6, waiting for transfers between devices, shift(): lax.ppermute(array, axis, [(i, (i + by) % extent) for i in range(extent)])  26.2 us
    ppermute x6, starting transfers between devices, shift(): lax.ppermute(array, axis, [(i, (i + by) % extent) for i in range(extent)])  16.8 us
    ppermute x16, starting transfers between devices, swap(): lax.ppermute(array, axis, [(i, i ^ 1 << bit) for i in range(lax.axis_size...  14.8 us
    another operation x4, other arithmetic, local(): near, far = (jnp.stack(near), jnp.stack(far))  4.27 us
    dynamic_slice x1, local copies, waits for them, and re-layouts, own_columns(): lax.dynamic_slice_in_dim(own, (row ^ delta) * cols * span, cols * span, 1)  3.7 us
  transfers between devices with their start and end apart: 22, of which 14 were waited for; matrix products, arithmetic and copies ran while one was open for 8% of the time, Pallas kernels for 16%

profile of v4, /device:TPU:0, one launch (start us, length us, event | category | flops | bytes accessed | tf_op | source)
XLA Modules:
  0.0 130.4 jit_solution(9480358906986227049)
XLA Ops:
  0.6 1.8 %masked.1 = bf16[2,384,256]{2,1,0:T(8,128)(2,1)} custom-call(s32[3]{0:T(128)} %pad_add_fusion.2.starts_ref, s32[1,48]{1,0:T(1,128)} %child_pattern_ref.1, s32[1,96]{1,0:T(1,128)} %parent_pattern_ref.1, bf16[384,256]{1,0:T(8,128)(2,1)} %bitcast.87, bf16[384,256]{1,0:T(8,128)(2,1)} %bitcast.88), custom_call_target="tpu_custom_call" | custom-call | tf_op jit(solution)/shard_map/masked/pallas_call | solution.py:36
  2.4 3.0 %collective-permute-start.9 = (bf16[2,384,256]{2,1,0:T(8,128)(2,1)}, bf16[2,384,256]{2,1,0:T(8,128)(2,1)S(1)}, u32[]{:S(2)}, u32[]{:S(2)}) collective-permute-start(bf16[2,384,256]{2,1,0:T(8,128)(2,1)} %masked.1), channel_id=1, source_target_pairs={{0,16},{16,0},{1,17},{17,1},{2,18},{18,2},{3,19},{19,3},{4,20},{20... | collective-permute-start | bytes 1179656 | tf_op jit(solution)/shard_map/ppermute | solution.py:12
  6.8 3.7 %dynamic-slice_bitcast_fusion.2 = (bf16[384,1536]{1,0:T(8,128)(2,1)S(1)}, bf16[384,1536]{1,0:T(8,128)(2,1)}, bf16[384,1536]{1,0:T(8,128)(2,1)S(1)}, bf16[384,1536]{1,0:T(8,128)(2,1)S(1)}) fusion(bf16[1,384,6144]{2,1,0:T(8,128)(2,1)} %param.11, s32[]{:T(128)S(6)} %select_n.46, s32[]{:T(128)S(6)} %select_n.45, s32[]{:T(128)S(6)} %select_n.48, s32[]{:T(128)S(6)} %select_n.47), kind=kLoop, calls=%fused_computation.7 | loop fusion | bytes 9437200 | tf_op jit(solution)/shard_map/dynamic_slice | solution.py:207
  10.8 8.1 %collective-permute-done = bf16[384,256]{1,0:T(8,128)(2,1)S(1)} collective-permute-done((bf16[384,256]{1,0:T(8,128)(2,1)S(1)}, bf16[384,256]{1,0:T(8,128)(2,1)S(1)}, u32[]{:S(2)}, u32[]{:S(2)}) %collective-permute-start) | collective-permute-done | bytes 196640 | tf_op jit(solution)/shard_map/ppermute | solution.py:12
  18.9 1.7 %collective-permute-start.19 = (bf16[384,4608]{1,0:T(8,128)(2,1)S(1)}, bf16[384,4608]{1,0:T(8,128)(2,1)}, u32[]{:S(2)}, u32[]{:S(2)}) collective-permute-start(bf16[384,4608]{1,0:T(8,128)(2,1)S(1)} %pad_maximum_fusion), channel_id=1, source_target_pairs={{0,16},{16,0},{1,17},{17,1},{2,18},{18,2},{3,19},{19,3},{4,20},{20... | collective-permute-start | bytes 10616840 | tf_op jit(solution)/shard_map/ppermute | solution.py:12
  20.7 1.6 %collective-permute-start.2 = (bf16[2,384,256]{2,1,0:T(8,128)(2,1)S(1)}, bf16[2,384,256]{2,1,0:T(8,128)(2,1)S(1)}, u32[]{:S(2)}, u32[]{:S(2)}) collective-permute-start(bf16[2,384,256]{2,1,0:T(8,128)(2,1)S(1)} %copy-done.1), channel_id=1, source_target_pairs={{0,1},{1,2},{2,3},{3,0},{4,5},{5,6},{6,7},{7,4},{8,9},{9,10},{10,1... | collective-permute-start | bytes 1179656 | tf_op jit(solution)/shard_map/ppermute | solution.py:17
  22.3 1.5 %collective-permute-start.1 = (bf16[2,384,256]{2,1,0:T(8,128)(2,1)S(1)}, bf16[2,384,256]{2,1,0:T(8,128)(2,1)S(1)}, u32[]{:S(2)}, u32[]{:S(2)}) collective-permute-start(bf16[2,384,256]{2,1,0:T(8,128)(2,1)S(1)} %copy-done.1), channel_id=1, source_target_pairs={{0,8},{4,12},{8,0},{12,4},{1,9},{5,13},{9,1},{13,5},{2,10},{6,14},... | collective-permute-start | bytes 1179656 | tf_op jit(solution)/shard_map/ppermute | solution.py:12
  23.8 2.2 %collective-permute-start.5 = (bf16[2,384,256]{2,1,0:T(8,128)(2,1)S(1)}, bf16[2,384,256]{2,1,0:T(8,128)(2,1)S(1)}, u32[]{:S(2)}, u32[]{:S(2)}) collective-permute-start(bf16[2,384,256]{2,1,0:T(8,128)(2,1)S(1)} %copy-done.1), channel_id=1, source_target_pairs={{0,3},{1,0},{2,1},{3,2},{4,7},{5,4},{6,5},{7,6},{8,11},{9,8},{10,9... | collective-permute-start | bytes 1179656 | tf_op jit(solution)/shard_map/ppermute | solution.py:17
  26.0 8.6 %collective-permute-done.2 = bf16[2,384,256]{2,1,0:T(8,128)(2,1)S(1)} collective-permute-done((bf16[2,384,256]{2,1,0:T(8,128)(2,1)S(1)}, bf16[2,384,256]{2,1,0:T(8,128)(2,1)S(1)}, u32[]{:S(2)}, u32[]{:S(2)}) %collective-permute-start.2) | collective-permute-done | bytes 393248 | tf_op jit(solution)/shard_map/ppermute | solution.py:17
  34.6 1.5 %collective-permute-start.3 = (bf16[2,384,256]{2,1,0:T(8,128)(2,1)S(1)}, bf16[2,384,256]{2,1,0:T(8,128)(2,1)S(1)}, u32[]{:S(2)}, u32[]{:S(2)}) collective-permute-start(bf16[2,384,256]{2,1,0:T(8,128)(2,1)S(1)} %collective-permute-done.2), channel_id=1, source_target_pairs={{0,8},{4,12},{8,0},{12,4},{1,9},{5,13},{9,1},{13,5},{2,10},{6,14},... | collective-permute-start | bytes 1179656 | tf_op jit(solution)/shard_map/ppermute | solution.py:12
  36.1 3.0 %collective-permute-start.11 = (bf16[2,384,256]{2,1,0:T(8,128)(2,1)S(1)}, bf16[2,384,256]{2,1,0:T(8,128)(2,1)S(1)}, u32[]{:S(2)}, u32[]{:S(2)}) collective-permute-start(bf16[2,384,256]{2,1,0:T(8,128)(2,1)S(1)} %collective-permute-done.9), channel_id=1, source_target_pairs={{0,1},{1,2},{2,3},{3,0},{4,5},{5,6},{6,7},{7,4},{8,9},{9,10},{10,1... | collective-permute-start | bytes 1179656 | tf_op jit(solution)/shard_map/ppermute | solution.py:17
  39.1 3.9 %collective-permute-done.5 = bf16[2,384,256]{2,1,0:T(8,128)(2,1)S(1)} collective-permute-done((bf16[2,384,256]{2,1,0:T(8,128)(2,1)S(1)}, bf16[2,384,256]{2,1,0:T(8,128)(2,1)S(1)}, u32[]{:S(2)}, u32[]{:S(2)}) %collective-permute-start.5) | collective-permute-done | bytes 393248 | tf_op jit(solution)/shard_map/ppermute | solution.py:17
  43.5 1.9 %collective-permute-done.3 = bf16[2,384,256]{2,1,0:T(8,128)(2,1)S(1)} collective-permute-done((bf16[2,384,256]{2,1,0:T(8,128)(2,1)S(1)}, bf16[2,384,256]{2,1,0:T(8,128)(2,1)S(1)}, u32[]{:S(2)}, u32[]{:S(2)}) %collective-permute-start.3) | collective-permute-done | bytes 393248 | tf_op jit(solution)/shard_map/ppermute | solution.py:12
  45.4 1.5 %collective-permute-start.6 = (bf16[2,384,256]{2,1,0:T(8,128)(2,1)S(1)}, bf16[2,384,256]{2,1,0:T(8,128)(2,1)S(1)}, u32[]{:S(2)}, u32[]{:S(2)}) collective-permute-start(bf16[2,384,256]{2,1,0:T(8,128)(2,1)S(1)} %collective-permute-done.5), channel_id=1, source_target_pairs={{0,8},{4,12},{8,0},{12,4},{1,9},{5,13},{9,1},{13,5},{2,10},{6,14},... | collective-permute-start | bytes 1179656 | tf_op jit(solution)/shard_map/ppermute | solution.py:12
  46.9 4.3 %collective-permute-done.11 = bf16[2,384,256]{2,1,0:T(8,128)(2,1)S(1)} collective-permute-done((bf16[2,384,256]{2,1,0:T(8,128)(2,1)S(1)}, bf16[2,384,256]{2,1,0:T(8,128)(2,1)S(1)}, u32[]{:S(2)}, u32[]{:S(2)}) %collective-permute-start.11) | collective-permute-done | bytes 393248 | tf_op jit(solution)/shard_map/ppermute | solution.py:17
  51.2 3.9 %collective-permute-start.15 = (bf16[2,384,256]{2,1,0:T(8,128)(2,1)S(1)}, bf16[2,384,256]{2,1,0:T(8,128)(2,1)S(1)}, u32[]{:S(2)}, u32[]{:S(2)}) collective-permute-start(bf16[2,384,256]{2,1,0:T(8,128)(2,1)S(1)} %collective-permute-done.9), channel_id=1, source_target_pairs={{0,3},{1,0},{2,1},{3,2},{4,7},{5,4},{6,5},{7,6},{8,11},{9,8},{10,9... | collective-permute-start | bytes 1179656 | tf_op jit(solution)/shard_map/ppermute | solution.py:17
  55.3 4.2 %collective-permute-done.4 = bf16[2,384,256]{2,1,0:T(8,128)(2,1)S(1)} collective-permute-done((bf16[2,384,256]{2,1,0:T(8,128)(2,1)S(1)}, bf16[2,384,256]{2,1,0:T(8,128)(2,1)S(1)}, u32[]{:S(2)}, u32[]{:S(2)}) %collective-permute-start.4) | collective-permute-done | bytes 393248 | tf_op jit(solution)/shard_map/ppermute | solution.py:17
  59.5 5.5 %collective-permute-start.13 = (bf16[2,384,256]{2,1,0:T(8,128)(2,1)S(1)}, bf16[2,384,256]{2,1,0:T(8,128)(2,1)S(1)}, u32[]{:S(2)}, u32[]{:S(2)}) collective-permute-start(bf16[2,384,256]{2,1,0:T(8,128)(2,1)S(1)} %collective-permute-done.11), channel_id=1, source_target_pairs={{0,1},{1,2},{2,3},{3,0},{4,5},{5,6},{6,7},{7,4},{8,9},{9,10},{10,1... | collective-permute-start | bytes 1179656 | tf_op jit(solution)/shard_map/ppermute | solution.py:17
  65.8 2.0 %collective-permute-done.15 = bf16[2,384,256]{2,1,0:T(8,128)(2,1)S(1)} collective-permute-done((bf16[2,384,256]{2,1,0:T(8,128)(2,1)S(1)}, bf16[2,384,256]{2,1,0:T(8,128)(2,1)S(1)}, u32[]{:S(2)}, u32[]{:S(2)}) %collective-permute-start.15) | collective-permute-done | bytes 393248 | tf_op jit(solution)/shard_map/ppermute | solution.py:17
  67.8 2.3 %collective-permute-done.12 = bf16[2,384,256]{2,1,0:T(8,128)(2,1)S(1)} collective-permute-done((bf16[2,384,256]{2,1,0:T(8,128)(2,1)S(1)}, bf16[2,384,256]{2,1,0:T(8,128)(2,1)S(1)}, u32[]{:S(2)}, u32[]{:S(2)}) %collective-permute-start.12) | collective-permute-done | bytes 393248 | tf_op jit(solution)/shard_map/ppermute | solution.py:12
  70.1 1.5 %collective-permute-start.16 = (bf16[2,384,256]{2,1,0:T(8,128)(2,1)S(1)}, bf16[2,384,256]{2,1,0:T(8,128)(2,1)S(1)}, u32[]{:S(2)}, u32[]{:S(2)}) collective-permute-start(bf16[2,384,256]{2,1,0:T(8,128)(2,1)S(1)} %collective-permute-done.15), channel_id=1, source_target_pairs={{0,8},{4,12},{8,0},{12,4},{1,9},{5,13},{9,1},{13,5},{2,10},{6,14},... | collective-permute-start | bytes 1179656 | tf_op jit(solution)/shard_map/ppermute | solution.py:12
  71.6 3.3 %collective-permute-done.13 = bf16[2,384,256]{2,1,0:T(8,128)(2,1)S(1)} collective-permute-done((bf16[2,384,256]{2,1,0:T(8,128)(2,1)S(1)}, bf16[2,384,256]{2,1,0:T(8,128)(2,1)S(1)}, u32[]{:S(2)}, u32[]{:S(2)}) %collective-permute-start.13) | collective-permute-done | bytes 393248 | tf_op jit(solution)/shard_map/ppermute | solution.py:17
  74.9 3.6 %collective-permute-done.7 = bf16[2,384,256]{2,1,0:T(8,128)(2,1)S(1)} collective-permute-done((bf16[2,384,256]{2,1,0:T(8,128)(2,1)S(1)}, bf16[2,384,256]{2,1,0:T(8,128)(2,1)S(1)}, u32[]{:S(2)}, u32[]{:S(2)}) %collective-permute-start.7) | collective-permute-done | bytes 393248 | tf_op jit(solution)/shard_map/ppermute | solution.py:12
  78.5 1.5 %collective-permute-start.14 = (bf16[2,384,256]{2,1,0:T(8,128)(2,1)S(1)}, bf16[2,384,256]{2,1,0:T(8,128)(2,1)S(1)}, u32[]{:S(2)}, u32[]{:S(2)}) collective-permute-start(bf16[2,384,256]{2,1,0:T(8,128)(2,1)S(1)} %collective-permute-done.13), channel_id=1, source_target_pairs={{0,8},{4,12},{8,0},{12,4},{1,9},{5,13},{9,1},{13,5},{2,10},{6,14},... | collective-permute-start | bytes 1179656 | tf_op jit(solution)/shard_map/ppermute | solution.py:12
  83.5 3.5 %collective-permute-done.16 = bf16[2,384,256]{2,1,0:T(8,128)(2,1)S(1)} collective-permute-done((bf16[2,384,256]{2,1,0:T(8,128)(2,1)S(1)}, bf16[2,384,256]{2,1,0:T(8,128)(2,1)S(1)}, u32[]{:S(2)}, u32[]{:S(2)}) %collective-permute-start.16) | collective-permute-done | bytes 393248 | tf_op jit(solution)/shard_map/ppermute | solution.py:12
  86.9 4.8 %collective-permute-done.14 = bf16[2,384,256]{2,1,0:T(8,128)(2,1)S(1)} collective-permute-done((bf16[2,384,256]{2,1,0:T(8,128)(2,1)S(1)}, bf16[2,384,256]{2,1,0:T(8,128)(2,1)S(1)}, u32[]{:S(2)}, u32[]{:S(2)}) %collective-permute-start.14) | collective-permute-done | bytes 393248 | tf_op jit(solution)/shard_map/ppermute | solution.py:12
  93.1 3.7 %collective-permute-done.19.other_ref = bf16[384,4608]{1,0:T(8,128)(2,1)} collective-permute-done((bf16[384,4608]{1,0:T(8,128)(2,1)S(1)}, bf16[384,4608]{1,0:T(8,128)(2,1)}, u32[]{:S(2)}, u32[]{:S(2)}) %collective-permute-start.19) | collective-permute-done | bytes 3538976 | tf_op jit(solution)/shard_map/ppermute | solution.py:12
  99.1 7.2 %assemble.4.rest_0_ = bf16[384,12288]{1,0:T(8,128)(2,1)} custom-call(s32[192]{0:T(256)S(1)} %reshape.48.table_ref, s32[4]{0:T(128)S(1)} %get-tuple-element.23.place_ref, bf16[3,384,256]{2,1,0:T(8,128)(2,1)S(1)} %pad_maximum_fusion.5.lefts_ref, bf16[4,2,384,256]{3,2,1,0:T(8,128)(2,1)} %pad_maximum_fusion.3.own_set_ref, ...), custom_call_target="tpu_custom_call" | custom-call | flops 1207959552 | bytes 10813440 | tf_op jit(solution)/shard_map/assemble/pallas_call | solution.py:147
  106.3 7.0 %assemble.5.rest_0_ = bf16[384,12288]{1,0:T(8,128)(2,1)} custom-call(s32[192]{0:T(256)S(1)} %reshape.48.table_ref, s32[4]{0:T(128)S(1)} %get-tuple-element.29.place_ref, bf16[3,384,256]{2,1,0:T(8,128)(2,1)S(1)} %pad_maximum_fusion.5.lefts_ref, bf16[4,2,384,256]{3,2,1,0:T(8,128)(2,1)} %collective-permute-done.20.own_set_ref, ...), custom_call_target="tpu_custom_call", output_to_operand_aliasing={{}: (8, {})} | custom-call | flops 1207959552 | bytes 10813440 | tf_op jit(solution)/shard_map/assemble/pallas_call | solution.py:147
  113.4 6.6 %assemble.6.rest_0_ = bf16[384,12288]{1,0:T(8,128)(2,1)} custom-call(s32[192]{0:T(256)S(1)} %reshape.48.table_ref, s32[4]{0:T(128)S(1)} %get-tuple-element.30.place_ref, bf16[3,384,256]{2,1,0:T(8,128)(2,1)S(1)} %pad_maximum_fusion.5.lefts_ref, bf16[4,2,384,256]{3,2,1,0:T(8,128)(2,1)S(1)} %pad_maximum_fusion.1.own_set_ref, ...), custom_call_target="tpu_custom_call", output_to_operand_aliasing={{}: (8, {})} | custom-call | flops 1207959552 | bytes 10813440 | tf_op jit(solution)/shard_map/assemble/pallas_call | solution.py:147
  119.9 3.4 %collective-permute-done.18.other_ref = bf16[384,1536]{1,0:T(8,128)(2,1)} collective-permute-done((bf16[384,1536]{1,0:T(8,128)(2,1)}, bf16[384,1536]{1,0:T(8,128)(2,1)}, u32[]{:S(2)}, u32[]{:S(2)}) %collective-permute-start.18) | collective-permute-done | bytes 1179680 | tf_op jit(solution)/shard_map/ppermute | solution.py:12
  123.3 7.0 %assemble.7 = bf16[384,12288]{1,0:T(8,128)(2,1)} custom-call(s32[192]{0:T(256)S(1)} %reshape.48.table_ref, s32[4]{0:T(128)S(1)} %get-tuple-element.31.place_ref, bf16[3,384,256]{2,1,0:T(8,128)(2,1)S(1)} %pad_maximum_fusion.5.lefts_ref, bf16[4,2,384,256]{3,2,1,0:T(8,128)(2,1)} %collective-permute-done.8.own_set_ref, ...), custom_call_target="tpu_custom_call", output_to_operand_aliasing={{}: (8, {})} | custom-call | flops 1207959552 | bytes 10813440 | tf_op jit(solution)/shard_map/assemble/pallas_call | solution.py:147
  (49 shorter events, 10.9 us)
Async XLA Ops:
  0.0 5.4 %copy-start = (f32[1,256,256]{2,1,0:T(8,128)S(1)}, f32[1,256,256]{2,1,0:T(8,128)}, u32[]{:S(2)}) copy-start(f32[1,256,256]{2,1,0:T(8,128)} %param.10) | copy-start | bytes 786436
  2.4 16.5 %collective-permute-start.9 = (bf16[2,384,256]{2,1,0:T(8,128)(2,1)}, bf16[2,384,256]{2,1,0:T(8,128)(2,1)S(1)}, u32[]{:S(2)}, u32[]{:S(2)}) collective-permute-start(bf16[2,384,256]{2,1,0:T(8,128)(2,1)} %masked.1), channel_id=1, source_target_pairs={{0,16},{16,0},{1,17},{17,1},{2,18},{18,2},{3,19},{19,3},{4,20},{20... | collective-permute-start | bytes 1179656 | tf_op jit(solution)/shard_map/ppermute | solution.py:12
  6.7 12.2 %collective-permute-start = (bf16[384,256]{1,0:T(8,128)(2,1)S(1)}, bf16[384,256]{1,0:T(8,128)(2,1)S(1)}, u32[]{:S(2)}, u32[]{:S(2)}) collective-permute-start(bf16[384,256]{1,0:T(8,128)(2,1)S(1)} %convolution_convert_fusion.1), channel_id=1, source_target_pairs={{0,16},{16,0},{1,17},{17,1},{2,18},{18,2},{3,19},{19,3},{4,20},{20... | collective-permute-start | bytes 589832 | tf_op jit(solution)/shard_map/ppermute | solution.py:12
  10.5 10.2 %copy-start.1 = (bf16[2,384,256]{2,1,0:T(8,128)(2,1)S(1)}, bf16[2,384,256]{2,1,0:T(8,128)(2,1)}, u32[]{:S(2)}) copy-start(bf16[2,384,256]{2,1,0:T(8,128)(2,1)} %masked.1) | copy-start | bytes 1179652
  10.5 54.8 %copy-start.2 = (f32[1,256,256]{2,1,0:T(8,128)S(1)}, f32[1,256,256]{2,1,0:T(8,128)}, u32[]{:S(2)}) copy-start(f32[1,256,256]{2,1,0:T(8,128)} %param.15) | copy-start | bytes 786436
  18.9 77.8 %collective-permute-start.19 = (bf16[384,4608]{1,0:T(8,128)(2,1)S(1)}, bf16[384,4608]{1,0:T(8,128)(2,1)}, u32[]{:S(2)}, u32[]{:S(2)}) collective-permute-start(bf16[384,4608]{1,0:T(8,128)(2,1)S(1)} %pad_maximum_fusion), channel_id=1, source_target_pairs={{0,16},{16,0},{1,17},{17,1},{2,18},{18,2},{3,19},{19,3},{4,20},{20... | collective-permute-start | bytes 10616840 | tf_op jit(solution)/shard_map/ppermute | solution.py:12
  20.7 13.9 %collective-permute-start.2 = (bf16[2,384,256]{2,1,0:T(8,128)(2,1)S(1)}, bf16[2,384,256]{2,1,0:T(8,128)(2,1)S(1)}, u32[]{:S(2)}, u32[]{:S(2)}) collective-permute-start(bf16[2,384,256]{2,1,0:T(8,128)(2,1)S(1)} %copy-done.1), channel_id=1, source_target_pairs={{0,1},{1,2},{2,3},{3,0},{4,5},{5,6},{6,7},{7,4},{8,9},{9,10},{10,1... | collective-permute-start | bytes 1179656 | tf_op jit(solution)/shard_map/ppermute | solution.py:17
  22.3 13.8 %collective-permute-start.1 = (bf16[2,384,256]{2,1,0:T(8,128)(2,1)S(1)}, bf16[2,384,256]{2,1,0:T(8,128)(2,1)S(1)}, u32[]{:S(2)}, u32[]{:S(2)}) collective-permute-start(bf16[2,384,256]{2,1,0:T(8,128)(2,1)S(1)} %copy-done.1), channel_id=1, source_target_pairs={{0,8},{4,12},{8,0},{12,4},{1,9},{5,13},{9,1},{13,5},{2,10},{6,14},... | collective-permute-start | bytes 1179656 | tf_op jit(solution)/shard_map/ppermute | solution.py:12
  23.8 19.2 %collective-permute-start.5 = (bf16[2,384,256]{2,1,0:T(8,128)(2,1)S(1)}, bf16[2,384,256]{2,1,0:T(8,128)(2,1)S(1)}, u32[]{:S(2)}, u32[]{:S(2)}) collective-permute-start(bf16[2,384,256]{2,1,0:T(8,128)(2,1)S(1)} %copy-done.1), channel_id=1, source_target_pairs={{0,3},{1,0},{2,1},{3,2},{4,7},{5,4},{6,5},{7,6},{8,11},{9,8},{10,9... | collective-permute-start | bytes 1179656 | tf_op jit(solution)/shard_map/ppermute | solution.py:17
  34.6 10.8 %collective-permute-start.3 = (bf16[2,384,256]{2,1,0:T(8,128)(2,1)S(1)}, bf16[2,384,256]{2,1,0:T(8,128)(2,1)S(1)}, u32[]{:S(2)}, u32[]{:S(2)}) collective-permute-start(bf16[2,384,256]{2,1,0:T(8,128)(2,1)S(1)} %collective-permute-done.2), channel_id=1, source_target_pairs={{0,8},{4,12},{8,0},{12,4},{1,9},{5,13},{9,1},{13,5},{2,10},{6,14},... | collective-permute-start | bytes 1179656 | tf_op jit(solution)/shard_map/ppermute | solution.py:12
  36.1 15.1 %collective-permute-start.11 = (bf16[2,384,256]{2,1,0:T(8,128)(2,1)S(1)}, bf16[2,384,256]{2,1,0:T(8,128)(2,1)S(1)}, u32[]{:S(2)}, u32[]{:S(2)}) collective-permute-start(bf16[2,384,256]{2,1,0:T(8,128)(2,1)S(1)} %collective-permute-done.9), channel_id=1, source_target_pairs={{0,1},{1,2},{2,3},{3,0},{4,5},{5,6},{6,7},{7,4},{8,9},{9,10},{10,1... | collective-permute-start | bytes 1179656 | tf_op jit(solution)/shard_map/ppermute | solution.py:17
  39.0 16.0 %collective-permute-start.10 = (bf16[2,384,256]{2,1,0:T(8,128)(2,1)S(1)}, bf16[2,384,256]{2,1,0:T(8,128)(2,1)S(1)}, u32[]{:S(2)}, u32[]{:S(2)}) collective-permute-start(bf16[2,384,256]{2,1,0:T(8,128)(2,1)S(1)} %collective-permute-done.9), channel_id=1, source_target_pairs={{0,8},{4,12},{8,0},{12,4},{1,9},{5,13},{9,1},{13,5},{2,10},{6,14},... | collective-permute-start | bytes 1179656 | tf_op jit(solution)/shard_map/ppermute | solution.py:12
  42.9 16.6 %collective-permute-start.4 = (bf16[2,384,256]{2,1,0:T(8,128)(2,1)S(1)}, bf16[2,384,256]{2,1,0:T(8,128)(2,1)S(1)}, u32[]{:S(2)}, u32[]{:S(2)}) collective-permute-start(bf16[2,384,256]{2,1,0:T(8,128)(2,1)S(1)} %collective-permute-done.2), channel_id=1, source_target_pairs={{0,1},{1,2},{2,3},{3,0},{4,5},{5,6},{6,7},{7,4},{8,9},{9,10},{10,1... | collective-permute-start | bytes 1179656 | tf_op jit(solution)/shard_map/ppermute | solution.py:17
  45.4 19.7 %collective-permute-start.6 = (bf16[2,384,256]{2,1,0:T(8,128)(2,1)S(1)}, bf16[2,384,256]{2,1,0:T(8,128)(2,1)S(1)}, u32[]{:S(2)}, u32[]{:S(2)}) collective-permute-start(bf16[2,384,256]{2,1,0:T(8,128)(2,1)S(1)} %collective-permute-done.5), channel_id=1, source_target_pairs={{0,8},{4,12},{8,0},{12,4},{1,9},{5,13},{9,1},{13,5},{2,10},{6,14},... | collective-permute-start | bytes 1179656 | tf_op jit(solution)/shard_map/ppermute | solution.py:12
  51.2 16.7 %collective-permute-start.15 = (bf16[2,384,256]{2,1,0:T(8,128)(2,1)S(1)}, bf16[2,384,256]{2,1,0:T(8,128)(2,1)S(1)}, u32[]{:S(2)}, u32[]{:S(2)}) collective-permute-start(bf16[2,384,256]{2,1,0:T(8,128)(2,1)S(1)} %collective-permute-done.9), channel_id=1, source_target_pairs={{0,3},{1,0},{2,1},{3,2},{4,7},{5,4},{6,5},{7,6},{8,11},{9,8},{10,9... | collective-permute-start | bytes 1179656 | tf_op jit(solution)/shard_map/ppermute | solution.py:17
  55.1 15.0 %collective-permute-start.12 = (bf16[2,384,256]{2,1,0:T(8,128)(2,1)S(1)}, bf16[2,384,256]{2,1,0:T(8,128)(2,1)S(1)}, u32[]{:S(2)}, u32[]{:S(2)}) collective-permute-start(bf16[2,384,256]{2,1,0:T(8,128)(2,1)S(1)} %collective-permute-done.11), channel_id=1, source_target_pairs={{0,8},{4,12},{8,0},{12,4},{1,9},{5,13},{9,1},{13,5},{2,10},{6,14},... | collective-permute-start | bytes 1179656 | tf_op jit(solution)/shard_map/ppermute | solution.py:12
  59.5 15.4 %collective-permute-start.13 = (bf16[2,384,256]{2,1,0:T(8,128)(2,1)S(1)}, bf16[2,384,256]{2,1,0:T(8,128)(2,1)S(1)}, u32[]{:S(2)}, u32[]{:S(2)}) collective-permute-start(bf16[2,384,256]{2,1,0:T(8,128)(2,1)S(1)} %collective-permute-done.11), channel_id=1, source_target_pairs={{0,1},{1,2},{2,3},{3,0},{4,5},{5,6},{6,7},{7,4},{8,9},{9,10},{10,1... | collective-permute-start | bytes 1179656 | tf_op jit(solution)/shard_map/ppermute | solution.py:17
  65.0 13.5 %collective-permute-start.7 = (bf16[2,384,256]{2,1,0:T(8,128)(2,1)S(1)}, bf16[2,384,256]{2,1,0:T(8,128)(2,1)S(1)}, u32[]{:S(2)}, u32[]{:S(2)}) collective-permute-start(bf16[2,384,256]{2,1,0:T(8,128)(2,1)S(1)} %collective-permute-done.4), channel_id=1, source_target_pairs={{0,8},{4,12},{8,0},{12,4},{1,9},{5,13},{9,1},{13,5},{2,10},{6,14},... | collective-permute-start | bytes 1179656 | tf_op jit(solution)/shard_map/ppermute | solution.py:12
  70.1 16.9 %collective-permute-start.16 = (bf16[2,384,256]{2,1,0:T(8,128)(2,1)S(1)}, bf16[2,384,256]{2,1,0:T(8,128)(2,1)S(1)}, u32[]{:S(2)}, u32[]{:S(2)}) collective-permute-start(bf16[2,384,256]{2,1,0:T(8,128)(2,1)S(1)} %collective-permute-done.15), channel_id=1, source_target_pairs={{0,8},{4,12},{8,0},{12,4},{1,9},{5,13},{9,1},{13,5},{2,10},{6,14},... | collective-permute-start | bytes 1179656 | tf_op jit(solution)/shard_map/ppermute | solution.py:12
  78.5 13.2 %collective-permute-start.14 = (bf16[2,384,256]{2,1,0:T(8,128)(2,1)S(1)}, bf16[2,384,256]{2,1,0:T(8,128)(2,1)S(1)}, u32[]{:S(2)}, u32[]{:S(2)}) collective-permute-start(bf16[2,384,256]{2,1,0:T(8,128)(2,1)S(1)} %collective-permute-done.13), channel_id=1, source_target_pairs={{0,8},{4,12},{8,0},{12,4},{1,9},{5,13},{9,1},{13,5},{2,10},{6,14},... | collective-permute-start | bytes 1179656 | tf_op jit(solution)/shard_map/ppermute | solution.py:12
  81.4 24.9 %collective-permute-start.20 = (bf16[4,2,384,256]{3,2,1,0:T(8,128)(2,1)}, bf16[4,2,384,256]{3,2,1,0:T(8,128)(2,1)}, u32[]{:S(2)}, u32[]{:S(2)}) collective-permute-start(bf16[4,2,384,256]{3,2,1,0:T(8,128)(2,1)} %pad_maximum_fusion.3.own_set_ref), channel_id=1, source_target_pairs={{0,4},{4,0},{8,12},{12,8},{1,5},{5,1},{9,13},{13,9},{2,6},{6,2},{1... | collective-permute-start | bytes 4718600 | tf_op jit(solution)/shard_map/ppermute | solution.py:12
  82.8 23.6 %collective-permute-start.21 = (bf16[4,2,384,256]{3,2,1,0:T(8,128)(2,1)}, bf16[4,2,384,256]{3,2,1,0:T(8,128)(2,1)}, u32[]{:S(2)}, u32[]{:S(2)}) collective-permute-start(bf16[4,2,384,256]{3,2,1,0:T(8,128)(2,1)} %pad_maximum_fusion.4.other_set_ref), channel_id=1, source_target_pairs={{0,4},{4,0},{8,12},{12,8},{1,5},{5,1},{9,13},{13,9},{2,6},{6,2},{1... | collective-permute-start | bytes 4718600 | tf_op jit(solution)/shard_map/ppermute | solution.py:12
  86.9 36.4 %collective-permute-start.8 = (bf16[4,2,384,256]{3,2,1,0:T(8,128)(2,1)S(1)}, bf16[4,2,384,256]{3,2,1,0:T(8,128)(2,1)}, u32[]{:S(2)}, u32[]{:S(2)}) collective-permute-start(bf16[4,2,384,256]{3,2,1,0:T(8,128)(2,1)S(1)} %pad_maximum_fusion.1.own_set_ref), channel_id=1, source_target_pairs={{0,4},{4,0},{8,12},{12,8},{1,5},{5,1},{9,13},{13,9},{2,6},{6,2},{1... | collective-permute-start | bytes 4718600 | tf_op jit(solution)/shard_map/ppermute | solution.py:12
  91.7 6.5 %copy-start.3 = (s32[2,48]{1,0:T(2,128)S(1)}, s32[2,48]{1,0:T(2,128)}, u32[]{:S(2)}) copy-start(s32[2,48]{1,0:T(2,128)} %param.13) | copy-start | bytes 1156
  93.1 30.2 %collective-permute-start.17 = (bf16[4,2,384,256]{3,2,1,0:T(8,128)(2,1)}, bf16[4,2,384,256]{3,2,1,0:T(8,128)(2,1)}, u32[]{:S(2)}, u32[]{:S(2)}) collective-permute-start(bf16[4,2,384,256]{3,2,1,0:T(8,128)(2,1)} %pad_maximum_fusion.2.other_set_ref), channel_id=1, source_target_pairs={{0,4},{4,0},{8,12},{12,8},{1,5},{5,1},{9,13},{13,9},{2,6},{6,2},{1... | collective-permute-start | bytes 4718600 | tf_op jit(solution)/shard_map/ppermute | solution.py:12
  96.8 26.5 %collective-permute-start.18 = (bf16[384,1536]{1,0:T(8,128)(2,1)}, bf16[384,1536]{1,0:T(8,128)(2,1)}, u32[]{:S(2)}, u32[]{:S(2)}) collective-permute-start(bf16[384,1536]{1,0:T(8,128)(2,1)} %get-tuple-element.26), channel_id=1, source_target_pairs={{0,16},{16,0},{1,17},{17,1},{2,18},{18,2},{3,19},{19,3},{4,20},{20... | collective-permute-start | bytes 3538952 | tf_op jit(solution)/shard_map/ppermute | solution.py:12
